TPU v7x, 256 devices: a whole 4x4x8 slice. The times are simulated.
256 devices in a mesh: seq: 8 (over x, core), level: 32 (over y, z).
Axes of the slice: x: 4, y: 4, z: 8, core: 2. Of those that a mesh axis runs over, the one named last changes fastest.
Arguments:
- states: float32 [64, 480, 64, 128], P('seq', 'level'), may hold values from -0.3 to 0.3
- xbc: bfloat16 [64, 8, 1792], P('seq', None, 'level'), may hold values from -1.796875 to 1.796875
- rates: float32 [64, 8, 24], P('seq'), may hold values from 0.02 to 0.8
- level_weights: float32 [64, 8, 480], P('seq', None, 'level'), may hold values from 0.1 to 1
- positions: int32 [64], P('seq'), may hold values from 0 to 1048567, as said below
- accepted: int32 [64], P('seq'), may hold values from 0 to 8
Outputs:
- outputs: bfloat16 [64, 8, 1536], P('seq', None, 'level')
- new_states: float32 [64, 480, 64, 128], P('seq', 'level')
- acceptance: float32 [], replicated
Inputs may be any that keep to these rules, and one draw needn't show every extreme that they name: `positions`: p + 8 stays below 2**20.
All inputs are finite; a program needn't handle non-finite values.
Results may differ from a plain program's by a relative error of at most 0.0019.
Values may be sent and summed in bfloat16 or wider, within the bound.
A program may use at most 64 MiB of HBM per device.

v0:
```python
import functools

import jax
import jax.numpy as jnp
from jax import lax
from jax.experimental import pallas as pl
from jax.experimental.pallas import tpu as pltpu
from jax.sharding import PartitionSpec as P

H = 24
P_SIZE = 64
N = 128
L = 20
K = 8
ROW = 8
OWN_IN = 56
OWN_OUT = 48
LOCAL = 15
BC_FIRST = 27
BC_SLOTS = 5
X_LOW, X_HIGH = -5, 2
MESH = pl.DeviceIdType.MESH
F32 = jnp.float32
BF16 = jnp.bfloat16


def first_head_of(d):
    return lax.rem(lax.div(LOCAL * d + L // 2, L), H)


def first_level_of(d):
    return lax.rem(LOCAL * d + L // 2, L)


def heads_of(d):
    return jnp.where(first_level_of(d) + LOCAL > L, 2, 1)


def value_offset(d, s):
    u = OWN_IN * s - P_SIZE * first_head_of(d)
    return jnp.where(u < -(H * P_SIZE) // 2, u + H * P_SIZE, u)


def needs_values(d, s):
    u = value_offset(d, s)
    return (s <= BC_FIRST) & (u > -OWN_IN) & (u < P_SIZE * heads_of(d))


def wrapped(d, devices):
    return lax.rem(d + devices, devices)


def as_int(x):
    return x.astype(jnp.int32)


def split_two(x):
    high = x.astype(BF16).astype(F32)
    return high, x - high


def kernel(
    devices,
    groups,
    states_ref,
    xbc_ref,
    rates_ref,
    weights_ref,
    pos_ref,
    acc_ref,
    out_ref,
    new_ref,
    share_ref,
    held,
    halves,
    made,
    padded,
    piece,
    bc,
    xs,
    low_send,
    low_recv,
    low_a,
    low_b,
    leave_c,
    stay_c,
    into_c,
    wide_w,
    cc,
    bb,
    xg,
    psend,
    pslots,
    counts,
    in_sem,
    new_sem,
    y_send,
    z_send,
    x_send,
    bc_recv,
    x_recv,
    low_sems,
    p_send,
    p_recv,
    n_send,
    n_recv,
):
    seqs = xbc_ref.shape[0]
    rows = seqs * K
    me = lax.axis_index("level")
    sq = lax.axis_index("seq")
    y, z = lax.div(me, ROW), lax.rem(me, ROW)
    columns = devices // ROW
    first_z = BC_FIRST - (columns - 1) * ROW
    has_slot = z >= first_z
    is_source = has_slot & (y == columns - 1)
    kind = lax.rem(me, 4)
    slot = jnp.maximum(z - first_z, 0)

    barrier = pltpu.get_barrier_semaphore()

    def greet(group, level):
        pl.semaphore_signal(barrier, inc=1, device_id=(group, level), device_id_type=MESH)

    for other in range(first_z, ROW):

        @pl.when(z != other)
        def _():
            greet(sq, y * ROW + other)

    @pl.when(has_slot & (y != columns - 1))
    def _():
        greet(sq, (columns - 1) * ROW + z)

    for gap in range(X_LOW, X_HIGH + 1):
        if gap != 0:
            source = wrapped(me + gap, devices)

            @pl.when(needs_values(me, source))
            def _():
                greet(sq, source)

    greet(sq, wrapped(me - 1, devices))

    @pl.when((kind == 1) | (kind == 2))
    def _():
        greet(sq, wrapped(me - 2, devices))

    @pl.when(kind == 2)
    def _():
        greet(sq, wrapped(me + 1, devices))

    for step in range(1, groups):
        greet(lax.rem(sq + step, groups), me)

    expected = 7 * as_int(has_slot) + (columns - 1) * as_int(is_source) + groups
    for gap in range(X_LOW, X_HIGH + 1):
        if gap != 0:
            expected = expected + as_int(needs_values(wrapped(me - gap, devices), me))
    expected = expected + as_int((kind == 0) | (kind == 3)) + as_int(kind == 3)

    def load(s):
        return pltpu.make_async_copy(states_ref.at[s], held.at[s], in_sem.at[s])

    for s in range(seqs):
        load(s).start()

    lane = lax.broadcasted_iota(jnp.int32, (rows, 128), 1)
    lower = lane < P_SIZE
    half_rows = rows // 2
    half_lane = lane[:half_rows]
    half_lower = half_lane < P_SIZE

    padded[...] = jnp.zeros_like(padded)
    padded[:, 0:OWN_IN] = xbc_ref[...].astype(F32).reshape(rows, OWN_IN)
    wide = padded[...]
    packed = jnp.where(half_lower, wide[:half_rows], pltpu.roll(wide[half_rows:], P_SIZE, 1))
    packed = packed.astype(BF16)
    piece[...] = packed
    xs[-X_LOW] = packed

    @pl.when(is_source)
    def _():
        bc[slot] = packed

    sub = lax.broadcasted_iota(jnp.int32, (seqs, 128), 0)
    pos_s = jnp.zeros((seqs, 128), jnp.int32)
    acc_s = jnp.zeros((seqs, 128), jnp.int32)
    for s in range(seqs):
        pos_s = jnp.where(sub == s, pos_ref[s], pos_s)
        acc_s = jnp.where(sub == s, acc_ref[s], acc_s)
    new_s = pos_s + acc_s
    changed = pos_s ^ new_s
    level_0 = first_level_of(me)
    split = jnp.minimum(L - level_0, LOCAL)
    levels = [lax.rem(level_0 + j, L) for j in range(LOCAL)] + [0]
    for j in range(LOCAL):
        occupied = (pos_s >> levels[j]) & 1
        above = changed >> levels[j]
        leave_c[j] = jnp.where((above >> 1) != 0, occupied, 0).astype(F32)

    block = LOCAL // 3
    halves[:, LOCAL * P_SIZE :, :] = jnp.zeros((seqs, P_SIZE, 2 * N), BF16)
    has_zero_in_a = level_0 == 0

    def gather_low(s, carry):
        load(s).wait()
        sums = []
        for part in range(3):
            total = None
            for j in range(part * block, (part + 1) * block):
                x = held[s, j * P_SIZE : (j + 1) * P_SIZE, :]
                high, low = split_two(x)
                halves[s, j * P_SIZE : (j + 1) * P_SIZE, 0:N] = high.astype(BF16)
                halves[s, j * P_SIZE : (j + 1) * P_SIZE, N : 2 * N] = low.astype(BF16)
                term = x * leave_c[j, pl.ds(s, 1), :]
                total = term if total is None else total + term
            sums.append(total)
        zero = jnp.zeros_like(sums[0])
        one_in_a, two_in_a = split > block, split > 2 * block
        in_a = sums[0] + jnp.where(one_in_a, sums[1], zero) + jnp.where(two_in_a, sums[2], zero)
        in_b = jnp.where(one_in_a, zero, sums[1]) + jnp.where(two_in_a, zero, sums[2])
        low_a[s] = in_a
        low_b[s] = in_b
        low_send[s] = jnp.where(has_zero_in_a, in_a, in_b).astype(BF16)
        return carry

    lax.fori_loop(0, seqs, gather_low, 0)

    taken_here = jnp.int32(0)
    for s in range(seqs):
        taken_here = taken_here + acc_ref[s]
    counts[sq] = jnp.full((8, 128), taken_here, jnp.int32).astype(F32)

    pl.semaphore_wait(barrier, expected)

    def remote(src, dst, send_sem, recv_sem, group, level):
        return pltpu.make_async_remote_copy(
            src_ref=src,
            dst_ref=dst,
            send_sem=send_sem,
            recv_sem=recv_sem,
            device_id=(group, level),
            device_id_type=MESH,
        )

    def y_copy(row):
        return remote(bc.at[slot], bc.at[slot], y_send.at[row], bc_recv.at[slot], sq, row * ROW + z)

    def z_copy(step):
        other = y * ROW + lax.rem(z + step, ROW)
        return remote(bc.at[slot], bc.at[slot], z_send.at[step], bc_recv.at[slot], sq, other)

    def x_copy(gap):
        target = wrapped(me - gap, devices)
        index = gap - X_LOW
        return remote(piece, xs.at[index], x_send.at[index], x_recv.at[index], sq, target)

    def low_copy():
        target = wrapped(me + 1, devices)
        return remote(low_send, low_recv, low_sems.at[0], low_sems.at[1], sq, target)

    def count_copy(step):
        return remote(
            counts.at[sq], counts.at[sq], n_send.at[step], n_recv.at[sq], lax.rem(sq + step, groups), me
        )

    def partial_copy(index, gap):
        target = wrapped(me + gap, devices)
        return remote(psend, pslots.at[index], p_send.at[index], p_recv.at[index], sq, target)

    sends_low = kind != 1
    gets_low = kind != 2
    gaps = [gap for gap in range(X_LOW, X_HIGH + 1) if gap != 0]
    near = (
        (0, 1, None, None),
        (1, 2, (kind == 0) | (kind == 3), (kind == 1) | (kind == 2)),
        (2, -1, kind == 3, kind == 2),
    )

    def when(cond, do):
        if cond is None:
            do()
        else:
            pl.when(cond)(do)

    @pl.when(is_source)
    def _():
        for row in range(columns - 1):
            y_copy(row).start()

    for gap in gaps:
        when(needs_values(wrapped(me - gap, devices), me), lambda: x_copy(gap).start())
    when(sends_low, lambda: low_copy().start())
    for step in range(1, groups):
        count_copy(step).start()

    head_lane = lax.broadcasted_iota(jnp.int32, (rows, H), 1)
    rates = rates_ref[...].reshape(rows, H)
    first_head = first_head_of(me)
    second_head = lax.rem(first_head + 1, H)
    row = lax.broadcasted_iota(jnp.int32, (rows, 128), 0)
    token = row & (K - 1)
    pos_rows = jnp.concatenate([jnp.full((K, 128), pos_ref[s], jnp.int32) for s in range(seqs)], 0)
    acc_rows = jnp.concatenate([jnp.full((K, 128), acc_ref[s], jnp.int32) for s in range(seqs)], 0)
    new_rows = pos_rows + acc_rows
    token_rows = pos_rows + token
    live = token < acc_rows

    def decays(head):
        rate = jnp.sum(jnp.where(head_lane == head, rates, 0.0), axis=1, keepdims=True)
        rate = jnp.broadcast_to(rate, (rows, 128))
        running = rate
        for by in (1, 2, 4):
            running = running + jnp.where(token >= by, pltpu.roll(running, by, 0), 0.0)
        cum = -running
        taken = -jnp.sum(jnp.where(live, rate, 0.0).reshape(seqs, K, 128), axis=1)
        taken_rows = jnp.broadcast_to(taken[:, None, :], (seqs, K, 128)).reshape(rows, 128)
        decay = jnp.where(live, jnp.exp(jnp.minimum(taken_rows - cum, 0.0)), 0.0)
        return cum, jnp.exp(cum), jnp.exp(taken), decay

    cum_a, grown_a, kept_a, decay_a = decays(first_head)
    cum_b, grown_b, kept_b, decay_b = decays(second_head)

    for j in range(LOCAL):
        in_a = j < split
        kept = jnp.where(in_a, kept_a, kept_b)
        occupied = (pos_s >> levels[j]) & 1
        new_occupied = (new_s >> levels[j]) & 1
        above = changed >> levels[j]
        stay_c[j] = jnp.where((above == 0) & (occupied == 1) & (new_occupied == 1), kept, 0.0)
        into_c[j] = jnp.where((above == 1) & (new_occupied == 1), kept, 0.0)

    weights = weights_ref[...].reshape(rows, LOCAL)
    local_lane = lax.broadcasted_iota(jnp.int32, (rows, LOCAL), 1)
    level_lane = lax.rem(level_0 + local_lane, L)
    weight_zero = jnp.sum(jnp.where(level_lane == 0, weights, 0.0), axis=1, keepdims=True)
    quads = (LOCAL + 1) // 2

    def of_lane(q):
        two = 2 * q + jnp.where(lower, 0, 1)
        return jnp.where(lower, levels[2 * q], levels[2 * q + 1]), two < split, two < LOCAL

    for q in range(quads):
        level, in_a, real = of_lane(q)
        first = jnp.broadcast_to(weights[:, 2 * q : 2 * q + 1], (rows, 128))
        if 2 * q + 1 < LOCAL:
            second = jnp.broadcast_to(weights[:, 2 * q + 1 : 2 * q + 2], (rows, 128))
        else:
            second = jnp.zeros((rows, 128), F32)
        occupied = ((pos_rows >> level) & 1) == 1
        grown = jnp.where(in_a, grown_a, grown_b)
        wide_w[q] = jnp.where(occupied & real, jnp.where(lower, first, second) * grown, 0.0)

    @pl.when(has_slot)
    def _():
        @pl.when(y != columns - 1)
        def _():
            remote(
                bc.at[slot], bc.at[slot], y_send.at[0], bc_recv.at[slot], sq, me
            ).wait_recv()

        for step in range(1, ROW):
            z_copy(step).start()

    for other in range(first_z, ROW):
        index = other - first_z

        @pl.when(z != other)
        def _():
            remote(
                bc.at[index], bc.at[index], y_send.at[0], bc_recv.at[index], sq, me
            ).wait_recv()

    got = [bc[i].astype(F32) for i in range(BC_SLOTS)]

    def vectors(first_feature):
        parts = []
        for r in range(2):
            part = jnp.zeros((half_rows, 128), F32)
            for i in range(BC_SLOTS):
                start = OWN_IN * (BC_FIRST + i) - first_feature
                if start > -OWN_IN and start < N:
                    moved = got[i]
                    by = (start - P_SIZE * r) % 128
                    if by:
                        moved = pltpu.roll(moved, by, 1)
                    part = jnp.where((half_lane >= start) & (half_lane < start + OWN_IN), moved, part)
            parts.append(part)
        return jnp.concatenate(parts, axis=0)

    in_vecs = vectors(H * P_SIZE)
    out_vecs = vectors(H * P_SIZE + N)
    c3 = out_vecs.reshape(seqs, K, N)
    c3 = jnp.concatenate([c3, jnp.zeros_like(c3)], axis=1).astype(BF16)
    cc[:, :, 0:N] = c3
    cc[:, :, N : 2 * N] = c3

    for gap in gaps:
        index = gap - X_LOW
        source = wrapped(me + gap, devices)
        when(
            needs_values(me, source),
            lambda: remote(
                piece, xs.at[index], x_send.at[index], x_recv.at[index], sq, me
            ).wait_recv(),
        )
    value_parts = []
    for r in range(2):
        part = jnp.zeros((half_rows, 128), F32)
        for gap in range(X_LOW, X_HIGH + 1):
            source = wrapped(me + gap, devices)
            start = value_offset(me, source)
            end = start + jnp.minimum(OWN_IN, H * P_SIZE - OWN_IN * source)
            wanted = needs_values(me, source)
            first = jnp.where(wanted, start, 128)
            by = lax.rem(start + 4 * H * P_SIZE - P_SIZE * r, 128)
            moved = pltpu.roll(xs[gap - X_LOW].astype(F32), by, 1)
            part = jnp.where((half_lane >= first) & (half_lane < end), moved, part)
        value_parts.append(part)
    values = jnp.concatenate(value_parts, axis=0)

    b16 = in_vecs.astype(BF16)
    scores = lax.dot_general(
        out_vecs.astype(BF16),
        jnp.concatenate([b16, b16], axis=0),
        (((1,), (1,)), ((), ())),
        preferred_element_type=F32,
    )
    cum_zero = jnp.where(has_zero_in_a, cum_a, cum_b)
    source_row = lane & (rows - 1)
    cum_across = jnp.sum(jnp.where(source_row == row, cum_zero, 0.0), axis=0, keepdims=True)
    before = ((source_row >> 3) == (row >> 3)) & (source_row <= row)
    mixing = jnp.where(before, jnp.exp(jnp.minimum(cum_zero - cum_across, 0.0)), 0.0) * scores
    high, low = split_two(mixing)
    v16 = values.astype(BF16)
    mixed = jnp.dot(
        jnp.where(lower, high, low).astype(BF16),
        jnp.concatenate([v16, v16], axis=0),
        preferred_element_type=F32,
    )
    zero_here = jnp.where(lower, 1, 0) == as_int(has_zero_in_a)
    psend[...] = jnp.where(zero_here, mixed * weight_zero, 0.0)

    lane8 = lane[:K]
    lower8 = lane8 < P_SIZE

    def read_out(s, carry):
        read = lax.dot_general(
            cc[s], halves[s], (((1,), (1,)), ((), ())), preferred_element_type=F32
        )
        sum_a = jnp.zeros((K, 128), F32)
        sum_b = jnp.zeros((K, 128), F32)
        at = pl.ds(pl.multiple_of(s * K, K), K)
        for q in range(quads):
            two = 2 * q + jnp.where(lower8, 0, 1)
            term = read[:K, q * 128 : (q + 1) * 128] * wide_w[q, at, :]
            sum_a = sum_a + jnp.where(two < split, term, 0.0)
            sum_b = sum_b + jnp.where(two < split, 0.0, term)
        sum_a = sum_a + pltpu.roll(sum_a, P_SIZE, 1)
        sum_b = sum_b + pltpu.roll(sum_b, P_SIZE, 1)
        psend[at, :] = psend[at, :] + jnp.where(lower8, sum_a, sum_b)
        return carry

    lax.fori_loop(0, seqs, read_out, 0)

    for index, gap, sends, _ in near:
        when(sends, lambda: partial_copy(index, gap).start())

    turned = pltpu.roll(values, P_SIZE, 1)
    values_a = jnp.where(lower, values, turned) * decay_a
    values_b = jnp.where(lower, turned, values) * decay_b
    b3 = in_vecs.reshape(seqs, K, N)
    bb[...] = jnp.concatenate([b3, b3], axis=1).astype(BF16)
    for q in range(quads):
        level, in_a, real = of_lane(q)
        until = new_rows >> level
        inside = ((until & 1) == 1) & ((token_rows >> level) + 1 == until) & live & real
        term = jnp.where(inside, jnp.where(in_a, values_a, values_b), 0.0)
        high, low = split_two(term)
        both = jnp.concatenate(
            [high.reshape(seqs, K, 128), low.reshape(seqs, K, 128)], axis=1
        )
        xg[:, :, q * 128 : (q + 1) * 128] = both.astype(BF16)

    when(gets_low, lambda: low_copy().wait_recv())

    def store(s):
        return pltpu.make_async_copy(made.at[s], new_ref.at[s], new_sem.at[s])

    def update(s, carry):
        tokens = lax.dot_general(
            xg[s], bb[s], (((0,), (0,)), ((), ())), preferred_element_type=F32
        )
        came = jnp.where(gets_low, low_recv[s].astype(F32), 0.0)
        merged_a = low_a[s] + came
        merged_b = low_b[s]
        merged = (
            merged_a,
            jnp.where(split > block, merged_a, merged_b),
            jnp.where(split > 2 * block, merged_a, merged_b),
        )
        for j in range(LOCAL):
            at = slice(j * P_SIZE, (j + 1) * P_SIZE)
            made[s, at, :] = (
                held[s, at, :] * stay_c[j, pl.ds(s, 1), :]
                + merged[j // block] * into_c[j, pl.ds(s, 1), :]
                + tokens[at, :]
            )
        store(s).start()
        return carry

    lax.fori_loop(0, seqs, update, 0)

    for index, gap, _, gets in near:
        when(
            gets,
            lambda: remote(
                psend, pslots.at[index], p_send.at[index], p_recv.at[index], sq, me
            ).wait_recv(),
        )
    total = jnp.zeros((rows, 128), F32)
    sources = [(None, 0, None)] + [(index, -gap, gets) for index, gap, _, gets in near]
    for index, gap, gets in sources:
        source = wrapped(me + gap, devices)
        offset = OWN_OUT * me - P_SIZE * first_head_of(source)
        offset = jnp.where(offset < -(H * P_SIZE) // 2, offset + H * P_SIZE, offset)
        offset = jnp.where(offset > (H * P_SIZE) // 2, offset - H * P_SIZE, offset)
        by = lax.rem(4 * H * P_SIZE - offset, 128)
        end = P_SIZE * heads_of(source)
        if gets is not None:
            end = jnp.where(gets, end, -(1 << 20))
        moved = pltpu.roll(psend[...] if index is None else pslots[index], by, 1)
        total = total + jnp.where((lane + offset >= 0) & (lane + offset < end), moved, 0.0)
    out_ref[...] = total.reshape(seqs, K, 128)[:, :, 0:OWN_OUT].astype(BF16)

    for step in range(1, groups):
        other = lax.rem(sq + step, groups)
        remote(
            counts.at[other], counts.at[other], n_send.at[step], n_recv.at[other], sq, me
        ).wait_recv()
    taken = jnp.sum(counts[...], axis=0)
    share_ref[...] = taken[0:1, 0:1] / (groups * seqs * K)

    @pl.when(is_source)
    def _():
        for r in range(columns - 1):
            y_copy(r).wait_send()

    @pl.when(has_slot)
    def _():
        for step in range(1, ROW):
            z_copy(step).wait_send()

    for gap in gaps:
        when(needs_values(wrapped(me - gap, devices), me), lambda: x_copy(gap).wait_send())
    when(sends_low, lambda: low_copy().wait_send())
    for step in range(1, groups):
        count_copy(step).wait_send()
    for index, gap, sends, _ in near:
        when(sends, lambda: partial_copy(index, gap).wait_send())
    for s in range(seqs):
        store(s).wait()


def on_device(states, xbc, rates, level_weights, positions, accepted):
    devices = lax.axis_size("level")
    groups = lax.axis_size("seq")
    seqs = states.shape[0]
    rows = seqs * K
    wide = LOCAL * P_SIZE
    padded_wide = (LOCAL + 1) * P_SIZE
    vmem = pl.BlockSpec(memory_space=pltpu.VMEM)
    smem = pl.BlockSpec(memory_space=pltpu.SMEM)
    anywhere = pl.BlockSpec(memory_space=pl.ANY)
    in_hbm = pl.BlockSpec(memory_space=pltpu.HBM)
    dma = pltpu.SemaphoreType.DMA
    x_slots = X_HIGH - X_LOW + 1
    outputs, new_states, share = pl.pallas_call(
        functools.partial(kernel, devices, groups),
        out_shape=(
            jax.ShapeDtypeStruct((seqs, K, OWN_OUT), BF16),
            jax.ShapeDtypeStruct((seqs, wide, N), F32),
            jax.ShapeDtypeStruct((1, 1), F32),
        ),
        in_specs=[in_hbm, vmem, vmem, vmem, smem, smem],
        out_specs=(vmem, anywhere, vmem),
        scratch_shapes=[
            pltpu.VMEM((seqs, wide, N), F32),
            pltpu.VMEM((seqs, padded_wide, 2 * N), BF16),
            pltpu.VMEM((seqs, wide, N), F32),
            pltpu.VMEM((rows, 128), F32),
            pltpu.VMEM((rows // 2, 128), BF16),
            pltpu.VMEM((BC_SLOTS, rows // 2, 128), BF16),
            pltpu.VMEM((x_slots, rows // 2, 128), BF16),
            pltpu.VMEM((seqs, P_SIZE, N), BF16),
            pltpu.VMEM((seqs, P_SIZE, N), BF16),
            pltpu.VMEM((seqs, P_SIZE, N), F32),
            pltpu.VMEM((seqs, P_SIZE, N), F32),
            pltpu.VMEM((LOCAL, seqs, 128), F32),
            pltpu.VMEM((LOCAL, seqs, 128), F32),
            pltpu.VMEM((LOCAL, seqs, 128), F32),
            pltpu.VMEM(((LOCAL + 1) // 2, rows, 128), F32),
            pltpu.VMEM((seqs, 2 * K, 2 * N), BF16),
            pltpu.VMEM((seqs, 2 * K, N), BF16),
            pltpu.VMEM((seqs, 2 * K, padded_wide), BF16),
            pltpu.VMEM((rows, 128), F32),
            pltpu.VMEM((3, rows, 128), F32),
            pltpu.VMEM((groups, 8, 128), F32),
            dma((seqs,)),
            dma((seqs,)),
            dma((devices // ROW,)),
            dma((ROW,)),
            dma((x_slots,)),
            dma((BC_SLOTS,)),
            dma((x_slots,)),
            dma((2,)),
            dma((3,)),
            dma((3,)),
            dma((groups,)),
            dma((groups,)),
        ],
        compiler_params=pltpu.CompilerParams(
            collective_id=0, has_side_effects=True, vmem_limit_bytes=40 << 20
        ),
    )(
        states.reshape(seqs, wide, N),
        xbc,
        rates,
        level_weights,
        positions,
        accepted,
    )
    return outputs, new_states.reshape(states.shape), share.reshape(())


def solution(mesh):
    in_specs = (
        P("seq", "level", None, None),
        P("seq", None, "level"),
        P("seq", None, None),
        P("seq", None, "level"),
        P("seq"),
        P("seq"),
    )
    out_specs = (P("seq", None, "level"), P("seq", "level", None, None), P())
    return jax.shard_map(
        on_device, mesh=mesh, in_specs=in_specs, out_specs=out_specs, check_vma=False
    )
```

profile of v0, /device:TPU:4, one launch (start us, length us, event | category | flops | bytes accessed | tf_op | source)
XLA Modules:
  0.0 38.4 jit_solution(7762269476487657585)
XLA Ops:
  0.6 0.0 copy-start
  0.6 2.1 %copy-done = f32[8,15,64,128]{3,2,1,0:T(8,128)S(1)} copy-done((f32[8,15,64,128]{3,2,1,0:T(8,128)S(1)}, f32[8,15,64,128]{3,2,1,0:T(8,128)}, u32[]{:S(2)}) %copy-start) | copy-done | bytes 3932184
  2.7 0.0 copy-start.1
  2.7 0.8 %copy-done.1 = f32[8,8,24]{2,1,0:T(8,128)S(1)} copy-done((f32[8,8,24]{2,1,0:T(8,128)S(1)}, f32[8,8,24]{2,1,0:T(8,128)}, u32[]{:S(2)}) %copy-start.1) | copy-done | bytes 6168
  3.5 0.0 copy-start.2
  3.5 0.8 %copy-done.2 = f32[8,8,15]{2,1,0:T(8,128)S(1)} copy-done((f32[8,8,15]{2,1,0:T(8,128)S(1)}, f32[8,8,15]{2,1,0:T(8,128)}, u32[]{:S(2)}) %copy-start.2) | copy-done | bytes 3864
  4.3 0.0 copy-start.3
  4.3 0.7 %copy-done.3 = bf16[8,8,56]{2,1,0:T(8,128)(2,1)S(1)} copy-done((bf16[8,8,56]{2,1,0:T(8,128)(2,1)S(1)}, bf16[8,8,56]{2,1,0:T(8,128)(2,1)}, u32[]{:S(2)}) %copy-start.3) | copy-done | bytes 7192
  5.0 0.0 copy-start.4
  5.0 0.7 %copy-done.4 = s32[8]{0:T(128)S(1)} copy-done((s32[8]{0:T(128)S(1)}, s32[8]{0:T(128)}, u32[]{:S(2)}) %copy-start.4) | copy-done | bytes 56
  5.6 0.0 copy-start.5
  5.6 0.7 %copy-done.5 = s32[8]{0:T(128)S(1)} copy-done((s32[8]{0:T(128)S(1)}, s32[8]{0:T(128)}, u32[]{:S(2)}) %copy-start.5) | copy-done | bytes 56
  6.3 27.7 %shard_map.85 = (bf16[8,8,48]{2,1,0:T(8,128)(2,1)S(1)}, f32[8,960,128]{2,1,0:T(8,128)S(1)}, f32[1,1]{1,0:T(1,128)}) custom-call(f32[8,960,128]{2,1,0:T(8,128)S(1)} %bitcast.3, bf16[8,8,56]{2,1,0:T(8,128)(2,1)S(1)} %copy-done.3, f32[8,8,24]{2,1,0:T(8,128)S(1)} %copy-done.1, f32[8,8,15]{2,1,0:T(8,128)S(1)} %copy-done.2, s32[8]{0:T(128)S(1)} %copy-done.4, ...), custom_call_target="tpu_custom_call" | custom-call | tf_op jit(solution)/shard_map/pallas_call | solution.py:579
  34.0 0.6 %copy.12 = bf16[8,8,48]{2,1,0:T(8,128)(2,1)} copy(bf16[8,8,48]{2,1,0:T(8,128)(2,1)S(1)} %get-tuple-element.12) | data formatting | bytes 12288
  34.6 1.9 %copy.13 = f32[8,15,64,128]{3,2,1,0:T(8,128)} copy(f32[8,15,64,128]{3,2,1,0:T(8,128)S(1)} %bitcast.4) | data formatting | bytes 7864320
Async XLA Ops:
  0.6 2.1 %copy-start = (f32[8,15,64,128]{3,2,1,0:T(8,128)S(1)}, f32[8,15,64,128]{3,2,1,0:T(8,128)}, u32[]{:S(2)}) copy-start(f32[8,15,64,128]{3,2,1,0:T(8,128)} %param.6) | copy-start | bytes 11796484
  2.7 0.8 %copy-start.1 = (f32[8,8,24]{2,1,0:T(8,128)S(1)}, f32[8,8,24]{2,1,0:T(8,128)}, u32[]{:S(2)}) copy-start(f32[8,8,24]{2,1,0:T(8,128)} %rates_ref.1) | copy-start | bytes 18436
  3.5 0.8 %copy-start.2 = (f32[8,8,15]{2,1,0:T(8,128)S(1)}, f32[8,8,15]{2,1,0:T(8,128)}, u32[]{:S(2)}) copy-start(f32[8,8,15]{2,1,0:T(8,128)} %weights_ref.1) | copy-start | bytes 11524
  4.3 0.7 %copy-start.3 = (bf16[8,8,56]{2,1,0:T(8,128)(2,1)S(1)}, bf16[8,8,56]{2,1,0:T(8,128)(2,1)}, u32[]{:S(2)}) copy-start(bf16[8,8,56]{2,1,0:T(8,128)(2,1)} %xbc_ref.1) | copy-start | bytes 21508
  5.0 0.7 %copy-start.4 = (s32[8]{0:T(128)S(1)}, s32[8]{0:T(128)}, u32[]{:S(2)}) copy-start(s32[8]{0:T(128)} %pos_ref.1) | copy-start | bytes 100
  5.6 0.7 %copy-start.5 = (s32[8]{0:T(128)S(1)}, s32[8]{0:T(128)}, u32[]{:S(2)}) copy-start(s32[8]{0:T(128)} %acc_ref.1) | copy-start | bytes 100
where the time goes:
time: 38.7 us; the launch traced here: 38.4 us
  Pallas kernels  27.7 us (72%)
  local copies, waits for them, and re-layouts  8.18 us (21%)
  between operations  2.47 us (6%)
    pallas_call x1, Pallas kernels, on_device(): pl.pallas_call(functools.partial(kernel, devices, groups), out_shape=(jax...  27.7 us
    unnamed x14, local copies, waits for them, and re-layouts  8.18 us

commit v1 on v0

--- a/solution.py
+++ b/solution.py
@@ -63,17 +63,21 @@
     devices,
     groups,
     states_ref,
+    xbc_in,
+    rates_in,
+    weights_in,
+    pos_in,
+    acc_in,
+    out_ref,
+    new_ref,
+    share_ref,
     xbc_ref,
     rates_ref,
     weights_ref,
     pos_ref,
     acc_ref,
-    out_ref,
-    new_ref,
-    share_ref,
     held,
     halves,
-    made,
     padded,
     piece,
     bc,
@@ -92,8 +96,8 @@
     psend,
     pslots,
     counts,
+    small_sem,
     in_sem,
-    new_sem,
     y_send,
     z_send,
     x_send,
@@ -117,6 +121,27 @@
     kind = lax.rem(me, 4)
     slot = jnp.maximum(z - first_z, 0)
 
+    small = [
+        pltpu.make_async_copy(src, dst, small_sem.at[i])
+        for i, (src, dst) in enumerate(
+            (
+                (xbc_in, xbc_ref),
+                (pos_in, pos_ref),
+                (acc_in, acc_ref),
+                (rates_in, rates_ref),
+                (weights_in, weights_ref),
+            )
+        )
+    ]
+
+    def load(s):
+        return pltpu.make_async_copy(states_ref.at[s], held.at[s], in_sem.at[s])
+
+    for copy in small:
+        copy.start()
+    for s in range(seqs):
+        load(s).start()
+
     barrier = pltpu.get_barrier_semaphore()
 
     def greet(group, level):
@@ -159,12 +184,6 @@
             expected = expected + as_int(needs_values(wrapped(me - gap, devices), me))
     expected = expected + as_int((kind == 0) | (kind == 3)) + as_int(kind == 3)
 
-    def load(s):
-        return pltpu.make_async_copy(states_ref.at[s], held.at[s], in_sem.at[s])
-
-    for s in range(seqs):
-        load(s).start()
-
     lane = lax.broadcasted_iota(jnp.int32, (rows, 128), 1)
     lower = lane < P_SIZE
     half_rows = rows // 2
@@ -172,6 +191,7 @@
     half_lower = half_lane < P_SIZE
 
     padded[...] = jnp.zeros_like(padded)
+    small[0].wait()
     padded[:, 0:OWN_IN] = xbc_ref[...].astype(F32).reshape(rows, OWN_IN)
     wide = padded[...]
     packed = jnp.where(half_lower, wide[:half_rows], pltpu.roll(wide[half_rows:], P_SIZE, 1))
@@ -183,6 +203,8 @@
     def _():
         bc[slot] = packed
 
+    small[1].wait()
+    small[2].wait()
     sub = lax.broadcasted_iota(jnp.int32, (seqs, 128), 0)
     pos_s = jnp.zeros((seqs, 128), jnp.int32)
     acc_s = jnp.zeros((seqs, 128), jnp.int32)
@@ -296,6 +318,8 @@
         count_copy(step).start()
 
     head_lane = lax.broadcasted_iota(jnp.int32, (rows, H), 1)
+    small[3].wait()
+    small[4].wait()
     rates = rates_ref[...].reshape(rows, H)
     first_head = first_head_of(me)
     second_head = lax.rem(first_head + 1, H)
@@ -485,9 +509,6 @@
 
     when(gets_low, lambda: low_copy().wait_recv())
 
-    def store(s):
-        return pltpu.make_async_copy(made.at[s], new_ref.at[s], new_sem.at[s])
-
     def update(s, carry):
         tokens = lax.dot_general(
             xg[s], bb[s], (((0,), (0,)), ((), ())), preferred_element_type=F32
@@ -502,12 +523,11 @@
         )
         for j in range(LOCAL):
             at = slice(j * P_SIZE, (j + 1) * P_SIZE)
-            made[s, at, :] = (
+            new_ref[s, at, :] = (
                 held[s, at, :] * stay_c[j, pl.ds(s, 1), :]
                 + merged[j // block] * into_c[j, pl.ds(s, 1), :]
                 + tokens[at, :]
             )
-        store(s).start()
         return carry
 
     lax.fori_loop(0, seqs, update, 0)
@@ -559,8 +579,6 @@
         count_copy(step).wait_send()
     for index, gap, sends, _ in near:
         when(sends, lambda: partial_copy(index, gap).wait_send())
-    for s in range(seqs):
-        store(s).wait()
 
 
 def on_device(states, xbc, rates, level_weights, positions, accepted):
@@ -571,8 +589,6 @@
     wide = LOCAL * P_SIZE
     padded_wide = (LOCAL + 1) * P_SIZE
     vmem = pl.BlockSpec(memory_space=pltpu.VMEM)
-    smem = pl.BlockSpec(memory_space=pltpu.SMEM)
-    anywhere = pl.BlockSpec(memory_space=pl.ANY)
     in_hbm = pl.BlockSpec(memory_space=pltpu.HBM)
     dma = pltpu.SemaphoreType.DMA
     x_slots = X_HIGH - X_LOW + 1
@@ -583,12 +599,16 @@
             jax.ShapeDtypeStruct((seqs, wide, N), F32),
             jax.ShapeDtypeStruct((1, 1), F32),
         ),
-        in_specs=[in_hbm, vmem, vmem, vmem, smem, smem],
-        out_specs=(vmem, anywhere, vmem),
+        in_specs=[in_hbm] * 6,
+        out_specs=(vmem, vmem, vmem),
         scratch_shapes=[
+            pltpu.VMEM(xbc.shape, BF16),
+            pltpu.VMEM(rates.shape, F32),
+            pltpu.VMEM(level_weights.shape, F32),
+            pltpu.SMEM(positions.shape, jnp.int32),
+            pltpu.SMEM(accepted.shape, jnp.int32),
             pltpu.VMEM((seqs, wide, N), F32),
             pltpu.VMEM((seqs, padded_wide, 2 * N), BF16),
-            pltpu.VMEM((seqs, wide, N), F32),
             pltpu.VMEM((rows, 128), F32),
             pltpu.VMEM((rows // 2, 128), BF16),
             pltpu.VMEM((BC_SLOTS, rows // 2, 128), BF16),
@@ -607,7 +627,7 @@
             pltpu.VMEM((rows, 128), F32),
             pltpu.VMEM((3, rows, 128), F32),
             pltpu.VMEM((groups, 8, 128), F32),
-            dma((seqs,)),
+            dma((5,)),
             dma((seqs,)),
             dma((devices // ROW,)),
             dma((ROW,)),
@@ -624,12 +644,17 @@
             collective_id=0, has_side_effects=True, vmem_limit_bytes=40 << 20
         ),
     )(
-        states.reshape(seqs, wide, N),
-        xbc,
-        rates,
-        level_weights,
-        positions,
-        accepted,
+        *[
+            pltpu.with_memory_space_constraint(x, pltpu.HBM)
+            for x in (
+                states.reshape(seqs, wide, N),
+                xbc,
+                rates,
+                level_weights,
+                positions,
+                accepted,
+            )
+        ]
     )
     return outputs, new_states.reshape(states.shape), share.reshape(())
 

time: 38.7 us -> 29.9 us (0.77)
  the two profiles are of different devices: /device:TPU:4 before, /device:TPU:32 now
where the time goes in v1:
time: 29.9 us; the launch traced here: 29.8 us
  Pallas kernels  25 us (84%)
  local copies, waits for them, and re-layouts  2.53 us (8%)
  between operations  2.33 us (8%)
    pallas_call x1, Pallas kernels, on_device(): pl.pallas_call(functools.partial(kernel, devices, groups), out_shape=(jax...  25 us
    unnamed x2, local copies, waits for them, and re-layouts  2.53 us

profile of v1, /device:TPU:32, one launch (start us, length us, event | category | flops | bytes accessed | tf_op | source)
XLA Modules:
  0.0 29.8 jit_solution(1546810411938451439)
XLA Ops:
  0.6 25.0 %shard_map.85 = (bf16[8,8,48]{2,1,0:T(8,128)(2,1)S(1)}, f32[8,960,128]{2,1,0:T(8,128)S(1)}, f32[1,1]{1,0:T(1,128)}) custom-call(f32[8,960,128]{2,1,0:T(8,128)} %bitcast.4, bf16[8,8,56]{2,1,0:T(8,128)(2,1)} %xbc_in.1, f32[8,8,24]{2,1,0:T(8,128)} %rates_in.1, f32[8,8,15]{2,1,0:T(8,128)} %weights_in.1, s32[8]{0:T(128)} %pos_in.1, s32[8]{0:T(128)} %acc_in.1), custom_call_target="tpu_custom_call" | custom-call | tf_op jit(solution)/shard_map/pallas_call | solution.py:595
  25.6 0.6 %copy.12 = bf16[8,8,48]{2,1,0:T(8,128)(2,1)} copy(bf16[8,8,48]{2,1,0:T(8,128)(2,1)S(1)} %get-tuple-element.12) | data formatting | bytes 12288
  26.2 1.9 %copy.13 = f32[8,15,64,128]{3,2,1,0:T(8,128)} copy(f32[8,15,64,128]{3,2,1,0:T(8,128)S(1)} %bitcast.3) | data formatting | bytes 7864320

commit v2 on v1

--- a/solution.py
+++ b/solution.py
@@ -90,6 +90,7 @@
     stay_c,
     into_c,
     wide_w,
+    parts,
     cc,
     bb,
     xg,
@@ -216,14 +217,86 @@
     level_0 = first_level_of(me)
     split = jnp.minimum(L - level_0, LOCAL)
     levels = [lax.rem(level_0 + j, L) for j in range(LOCAL)] + [0]
+    block = LOCAL // 3
+    one_in_a, two_in_a = split > block, split > 2 * block
+    has_zero_in_a = level_0 == 0
+
+    taken_here = jnp.int32(0)
+    for s in range(seqs):
+        taken_here = taken_here + acc_ref[s]
+    counts[sq] = jnp.full((8, 128), taken_here, jnp.int32).astype(F32)
+
+    pl.semaphore_wait(barrier, expected)
+
+    def remote(src, dst, send_sem, recv_sem, group, level):
+        return pltpu.make_async_remote_copy(
+            src_ref=src,
+            dst_ref=dst,
+            send_sem=send_sem,
+            recv_sem=recv_sem,
+            device_id=(group, level),
+            device_id_type=MESH,
+        )
+
+    def y_copy(row):
+        return remote(bc.at[slot], bc.at[slot], y_send.at[row], bc_recv.at[slot], sq, row * ROW + z)
+
+    def z_copy(step):
+        other = y * ROW + lax.rem(z + step, ROW)
+        return remote(bc.at[slot], bc.at[slot], z_send.at[step], bc_recv.at[slot], sq, other)
+
+    def x_copy(gap):
+        target = wrapped(me - gap, devices)
+        index = gap - X_LOW
+        return remote(piece, xs.at[index], x_send.at[index], x_recv.at[index], sq, target)
+
+    def low_copy():
+        target = wrapped(me + 1, devices)
+        return remote(low_send, low_recv, low_sems.at[0], low_sems.at[1], sq, target)
+
+    def count_copy(step):
+        return remote(
+            counts.at[sq], counts.at[sq], n_send.at[step], n_recv.at[sq], lax.rem(sq + step, groups), me
+        )
+
+    def partial_copy(index, gap):
+        target = wrapped(me + gap, devices)
+        return remote(psend.at[index], pslots.at[index], p_send.at[index], p_recv.at[index], sq, target)
+
+    sends_low = kind != 1
+    gets_low = kind != 2
+    gaps = [gap for gap in range(X_LOW, X_HIGH + 1) if gap != 0]
+    near = (
+        (0, 2, (kind == 0) | (kind == 3), (kind == 1) | (kind == 2)),
+        (1, 1, None, None),
+        (2, -1, kind == 3, kind == 2),
+    )
+
+    def when(cond, do):
+        if cond is None:
+            do()
+        else:
+            pl.when(cond)(do)
+
+    z_steps = (4, 3, 5, 2, 6, 1, 7)
+
+    @pl.when(is_source)
+    def _():
+        for r in range(columns - 1):
+            y_copy(r).start()
+        for step in z_steps:
+            z_copy(step).start()
+
+    for gap in gaps:
+        when(needs_values(wrapped(me - gap, devices), me), lambda: x_copy(gap).start())
+    for step in range(1, groups):
+        count_copy(step).start()
+
+
     for j in range(LOCAL):
         occupied = (pos_s >> levels[j]) & 1
         above = changed >> levels[j]
         leave_c[j] = jnp.where((above >> 1) != 0, occupied, 0).astype(F32)
-
-    block = LOCAL // 3
-    halves[:, LOCAL * P_SIZE :, :] = jnp.zeros((seqs, P_SIZE, 2 * N), BF16)
-    has_zero_in_a = level_0 == 0
 
     def gather_low(s, carry):
         load(s).wait()
@@ -239,7 +312,6 @@
                 total = term if total is None else total + term
             sums.append(total)
         zero = jnp.zeros_like(sums[0])
-        one_in_a, two_in_a = split > block, split > 2 * block
         in_a = sums[0] + jnp.where(one_in_a, sums[1], zero) + jnp.where(two_in_a, sums[2], zero)
         in_b = jnp.where(one_in_a, zero, sums[1]) + jnp.where(two_in_a, zero, sums[2])
         low_a[s] = in_a
@@ -249,73 +321,13 @@
 
     lax.fori_loop(0, seqs, gather_low, 0)
 
-    taken_here = jnp.int32(0)
-    for s in range(seqs):
-        taken_here = taken_here + acc_ref[s]
-    counts[sq] = jnp.full((8, 128), taken_here, jnp.int32).astype(F32)
-
-    pl.semaphore_wait(barrier, expected)
-
-    def remote(src, dst, send_sem, recv_sem, group, level):
-        return pltpu.make_async_remote_copy(
-            src_ref=src,
-            dst_ref=dst,
-            send_sem=send_sem,
-            recv_sem=recv_sem,
-            device_id=(group, level),
-            device_id_type=MESH,
-        )
-
-    def y_copy(row):
-        return remote(bc.at[slot], bc.at[slot], y_send.at[row], bc_recv.at[slot], sq, row * ROW + z)
-
-    def z_copy(step):
-        other = y * ROW + lax.rem(z + step, ROW)
-        return remote(bc.at[slot], bc.at[slot], z_send.at[step], bc_recv.at[slot], sq, other)
-
-    def x_copy(gap):
-        target = wrapped(me - gap, devices)
-        index = gap - X_LOW
-        return remote(piece, xs.at[index], x_send.at[index], x_recv.at[index], sq, target)
-
-    def low_copy():
-        target = wrapped(me + 1, devices)
-        return remote(low_send, low_recv, low_sems.at[0], low_sems.at[1], sq, target)
-
-    def count_copy(step):
-        return remote(
-            counts.at[sq], counts.at[sq], n_send.at[step], n_recv.at[sq], lax.rem(sq + step, groups), me
-        )
-
-    def partial_copy(index, gap):
-        target = wrapped(me + gap, devices)
-        return remote(psend, pslots.at[index], p_send.at[index], p_recv.at[index], sq, target)
-
-    sends_low = kind != 1
-    gets_low = kind != 2
-    gaps = [gap for gap in range(X_LOW, X_HIGH + 1) if gap != 0]
-    near = (
-        (0, 1, None, None),
-        (1, 2, (kind == 0) | (kind == 3), (kind == 1) | (kind == 2)),
-        (2, -1, kind == 3, kind == 2),
-    )
-
-    def when(cond, do):
-        if cond is None:
-            do()
-        else:
-            pl.when(cond)(do)
-
-    @pl.when(is_source)
+    when(sends_low, lambda: low_copy().start())
+
+    @pl.when(has_slot & (y != columns - 1))
     def _():
-        for row in range(columns - 1):
-            y_copy(row).start()
-
-    for gap in gaps:
-        when(needs_values(wrapped(me - gap, devices), me), lambda: x_copy(gap).start())
-    when(sends_low, lambda: low_copy().start())
-    for step in range(1, groups):
-        count_copy(step).start()
+        remote(bc.at[slot], bc.at[slot], y_send.at[0], bc_recv.at[slot], sq, me).wait_recv()
+        for step in z_steps:
+            z_copy(step).start()
 
     head_lane = lax.broadcasted_iota(jnp.int32, (rows, H), 1)
     small[3].wait()
@@ -365,27 +377,17 @@
         two = 2 * q + jnp.where(lower, 0, 1)
         return jnp.where(lower, levels[2 * q], levels[2 * q + 1]), two < split, two < LOCAL
 
-    for q in range(quads):
-        level, in_a, real = of_lane(q)
-        first = jnp.broadcast_to(weights[:, 2 * q : 2 * q + 1], (rows, 128))
-        if 2 * q + 1 < LOCAL:
-            second = jnp.broadcast_to(weights[:, 2 * q + 1 : 2 * q + 2], (rows, 128))
-        else:
-            second = jnp.zeros((rows, 128), F32)
-        occupied = ((pos_rows >> level) & 1) == 1
-        grown = jnp.where(in_a, grown_a, grown_b)
-        wide_w[q] = jnp.where(occupied & real, jnp.where(lower, first, second) * grown, 0.0)
-
-    @pl.when(has_slot)
-    def _():
-        @pl.when(y != columns - 1)
-        def _():
-            remote(
-                bc.at[slot], bc.at[slot], y_send.at[0], bc_recv.at[slot], sq, me
-            ).wait_recv()
-
-        for step in range(1, ROW):
-            z_copy(step).start()
+    padded[:, 0:LOCAL] = weights
+    here = lane < LOCAL
+    level = level_0 + jnp.where(here, lane, 0)
+    level = jnp.where(level >= L, level - L, level)
+    shown = here & (((pos_rows >> level) & 1) == 1)
+    by_token = jnp.where(shown, padded[...] * jnp.where(lane < split, grown_a, grown_b), 0.0)
+    by_level = jnp.transpose(jnp.concatenate([by_token, jnp.zeros_like(by_token)], axis=0))
+    by_level = by_level[: LOCAL + 1]
+    for s in range(seqs):
+        wide_w[s] = jnp.where((lane[: LOCAL + 1] >> 3) == s, by_level, 0.0)
+    parts[...] = jnp.zeros_like(parts)
 
     for other in range(first_z, ROW):
         index = other - first_z
@@ -399,7 +401,7 @@
     got = [bc[i].astype(F32) for i in range(BC_SLOTS)]
 
     def vectors(first_feature):
-        parts = []
+        pair = []
         for r in range(2):
             part = jnp.zeros((half_rows, 128), F32)
             for i in range(BC_SLOTS):
@@ -410,15 +412,15 @@
                     if by:
                         moved = pltpu.roll(moved, by, 1)
                     part = jnp.where((half_lane >= start) & (half_lane < start + OWN_IN), moved, part)
-            parts.append(part)
-        return jnp.concatenate(parts, axis=0)
+            pair.append(part)
+        return jnp.concatenate(pair, axis=0)
 
     in_vecs = vectors(H * P_SIZE)
     out_vecs = vectors(H * P_SIZE + N)
-    c3 = out_vecs.reshape(seqs, K, N)
-    c3 = jnp.concatenate([c3, jnp.zeros_like(c3)], axis=1).astype(BF16)
-    cc[:, :, 0:N] = c3
-    cc[:, :, N : 2 * N] = c3
+    across = jnp.transpose(jnp.concatenate([out_vecs, jnp.zeros_like(out_vecs)], axis=0))
+    across = across.astype(BF16)
+    cc[0:N, :] = across
+    cc[N : 2 * N, :] = across
 
     for gap in gaps:
         index = gap - X_LOW
@@ -464,32 +466,44 @@
         preferred_element_type=F32,
     )
     zero_here = jnp.where(lower, 1, 0) == as_int(has_zero_in_a)
-    psend[...] = jnp.where(zero_here, mixed * weight_zero, 0.0)
-
-    lane8 = lane[:K]
-    lower8 = lane8 < P_SIZE
+    drafts = jnp.where(zero_here, mixed * weight_zero, 0.0)
 
     def read_out(s, carry):
-        read = lax.dot_general(
-            cc[s], halves[s], (((1,), (1,)), ((), ())), preferred_element_type=F32
-        )
-        sum_a = jnp.zeros((K, 128), F32)
-        sum_b = jnp.zeros((K, 128), F32)
-        at = pl.ds(pl.multiple_of(s * K, K), K)
-        for q in range(quads):
-            two = 2 * q + jnp.where(lower8, 0, 1)
-            term = read[:K, q * 128 : (q + 1) * 128] * wide_w[q, at, :]
-            sum_a = sum_a + jnp.where(two < split, term, 0.0)
-            sum_b = sum_b + jnp.where(two < split, 0.0, term)
-        sum_a = sum_a + pltpu.roll(sum_a, P_SIZE, 1)
-        sum_b = sum_b + pltpu.roll(sum_b, P_SIZE, 1)
-        psend[at, :] = psend[at, :] + jnp.where(lower8, sum_a, sum_b)
+        size = block * P_SIZE
+        for part in range(3):
+            read = jnp.dot(
+                halves[s, part * size : (part + 1) * size, :], cc[...], preferred_element_type=F32
+            )
+            total = parts[part]
+            for i in range(block):
+                j = part * block + i
+                total = total + read[i * P_SIZE : (i + 1) * P_SIZE, :] * wide_w[s, j : j + 1, :]
+            parts[part] = total
         return carry
 
-    lax.fori_loop(0, seqs, read_out, 0)
-
+    lax.fori_loop(0, seqs, read_out, 0, unroll=2)
+
+    zero = jnp.zeros((P_SIZE, 128), F32)
+    in_a = parts[0] + jnp.where(one_in_a, parts[1], zero) + jnp.where(two_in_a, parts[2], zero)
+    in_b = jnp.where(one_in_a, zero, parts[1]) + jnp.where(two_in_a, zero, parts[2])
+    readout = jnp.transpose(jnp.concatenate([in_a, in_b], axis=0))[:rows]
+    features = readout + drafts
+    held_end = P_SIZE * heads_of(me)
+
+    def packed_for(gap):
+        offset = OWN_OUT * wrapped(me + gap, devices) - P_SIZE * first_head
+        offset = jnp.where(offset < -(H * P_SIZE) // 2, offset + H * P_SIZE, offset)
+        offset = jnp.where(offset > (H * P_SIZE) // 2, offset - H * P_SIZE, offset)
+        moved = pltpu.roll(features, lax.rem(4 * H * P_SIZE - offset, 128), 1)
+        wanted = (lane < OWN_OUT) & (lane + offset >= 0) & (lane + offset < held_end)
+        moved = jnp.where(wanted, moved, 0.0)
+        return moved[:half_rows] + pltpu.roll(moved[half_rows:], P_SIZE, 1)
+
+    for index, gap, _, _ in near:
+        psend[index] = packed_for(gap)
     for index, gap, sends, _ in near:
         when(sends, lambda: partial_copy(index, gap).start())
+    own = packed_for(0)
 
     turned = pltpu.roll(values, P_SIZE, 1)
     values_a = jnp.where(lower, values, turned) * decay_a
@@ -536,22 +550,14 @@
         when(
             gets,
             lambda: remote(
-                psend, pslots.at[index], p_send.at[index], p_recv.at[index], sq, me
+                psend.at[index], pslots.at[index], p_send.at[index], p_recv.at[index], sq, me
             ).wait_recv(),
         )
-    total = jnp.zeros((rows, 128), F32)
-    sources = [(None, 0, None)] + [(index, -gap, gets) for index, gap, _, gets in near]
-    for index, gap, gets in sources:
-        source = wrapped(me + gap, devices)
-        offset = OWN_OUT * me - P_SIZE * first_head_of(source)
-        offset = jnp.where(offset < -(H * P_SIZE) // 2, offset + H * P_SIZE, offset)
-        offset = jnp.where(offset > (H * P_SIZE) // 2, offset - H * P_SIZE, offset)
-        by = lax.rem(4 * H * P_SIZE - offset, 128)
-        end = P_SIZE * heads_of(source)
-        if gets is not None:
-            end = jnp.where(gets, end, -(1 << 20))
-        moved = pltpu.roll(psend[...] if index is None else pslots[index], by, 1)
-        total = total + jnp.where((lane + offset >= 0) & (lane + offset < end), moved, 0.0)
+    total = own
+    for index, _, _, gets in near:
+        came = pslots[index]
+        total = total + (came if gets is None else jnp.where(gets, came, 0.0))
+    total = jnp.concatenate([total, pltpu.roll(total, P_SIZE, 1)], axis=0)
     out_ref[...] = total.reshape(seqs, K, 128)[:, :, 0:OWN_OUT].astype(BF16)
 
     for step in range(1, groups):
@@ -579,6 +585,16 @@
         count_copy(step).wait_send()
     for index, gap, sends, _ in near:
         when(sends, lambda: partial_copy(index, gap).wait_send())
+
+
+def flush(new_in, out_in, new_out, out_out, sems):
+    pieces = new_in.shape[0]
+    copies = [pltpu.make_async_copy(out_in, out_out, sems.at[pieces])]
+    copies += [pltpu.make_async_copy(new_in.at[s], new_out.at[s], sems.at[s]) for s in range(pieces)]
+    for copy in copies:
+        copy.start()
+    for copy in copies:
+        copy.wait()
 
 
 def on_device(states, xbc, rates, level_weights, positions, accepted):
@@ -608,7 +624,7 @@
             pltpu.SMEM(positions.shape, jnp.int32),
             pltpu.SMEM(accepted.shape, jnp.int32),
             pltpu.VMEM((seqs, wide, N), F32),
-            pltpu.VMEM((seqs, padded_wide, 2 * N), BF16),
+            pltpu.VMEM((seqs, wide, 2 * N), BF16),
             pltpu.VMEM((rows, 128), F32),
             pltpu.VMEM((rows // 2, 128), BF16),
             pltpu.VMEM((BC_SLOTS, rows // 2, 128), BF16),
@@ -620,12 +636,13 @@
             pltpu.VMEM((LOCAL, seqs, 128), F32),
             pltpu.VMEM((LOCAL, seqs, 128), F32),
             pltpu.VMEM((LOCAL, seqs, 128), F32),
-            pltpu.VMEM(((LOCAL + 1) // 2, rows, 128), F32),
-            pltpu.VMEM((seqs, 2 * K, 2 * N), BF16),
+            pltpu.VMEM((seqs, LOCAL + 1, 128), F32),
+            pltpu.VMEM((3, P_SIZE, 128), F32),
+            pltpu.VMEM((2 * N, 128), BF16),
             pltpu.VMEM((seqs, 2 * K, N), BF16),
             pltpu.VMEM((seqs, 2 * K, padded_wide), BF16),
-            pltpu.VMEM((rows, 128), F32),
-            pltpu.VMEM((3, rows, 128), F32),
+            pltpu.VMEM((3, rows // 2, 128), F32),
+            pltpu.VMEM((3, rows // 2, 128), F32),
             pltpu.VMEM((groups, 8, 128), F32),
             dma((5,)),
             dma((seqs,)),
@@ -656,6 +673,18 @@
             )
         ]
     )
+    anywhere = pl.BlockSpec(memory_space=pl.ANY)
+    new_states, outputs = pl.pallas_call(
+        flush,
+        out_shape=(
+            jax.ShapeDtypeStruct(new_states.shape, F32),
+            jax.ShapeDtypeStruct(outputs.shape, BF16),
+        ),
+        in_specs=[anywhere, anywhere],
+        out_specs=(in_hbm, in_hbm),
+        scratch_shapes=[dma((seqs + 1,))],
+        compiler_params=pltpu.CompilerParams(vmem_limit_bytes=4 << 20),
+    )(new_states, outputs)
     return outputs, new_states.reshape(states.shape), share.reshape(())
 
 

time: 29.9 us -> 28.6 us (0.957)
  the two profiles are of different devices: /device:TPU:32 before, /device:TPU:10 now
where the time goes in v2:
time: 28.6 us; the launch traced here: 28.2 us
  Pallas kernels  25.8 us (90%)
  between operations  2.41 us (8%)
    pallas_call x1, Pallas kernels, on_device(): pl.pallas_call(functools.partial(kernel, devices, groups), out_shape=(jax...  23.8 us
    pallas_call x1, Pallas kernels, on_device(): pl.pallas_call(flush, out_shape=(jax.ShapeDtypeStruct(new_states.shape, F...  2 us

profile of v2, /device:TPU:10, one launch (start us, length us, event | category | flops | bytes accessed | tf_op | source)
XLA Modules:
  0.0 28.2 jit_solution(10539942419294936600)
XLA Ops:
  0.6 23.8 %shard_map.85 = (bf16[8,8,48]{2,1,0:T(8,128)(2,1)S(1)}, f32[8,960,128]{2,1,0:T(8,128)S(1)}, f32[1,1]{1,0:T(1,128)}) custom-call(f32[8,960,128]{2,1,0:T(8,128)} %bitcast.3, bf16[8,8,56]{2,1,0:T(8,128)(2,1)} %xbc_in.1, f32[8,8,24]{2,1,0:T(8,128)} %rates_in.1, f32[8,8,15]{2,1,0:T(8,128)} %weights_in.1, s32[8]{0:T(128)} %pos_in.1, s32[8]{0:T(128)} %acc_in.1), custom_call_target="tpu_custom_call" | custom-call | tf_op jit(solution)/shard_map/pallas_call | solution.py:611
  24.5 2.0 %shard_map.86 = (f32[8,960,128]{2,1,0:T(8,128)}, bf16[8,8,48]{2,1,0:T(8,128)(2,1)}) custom-call(f32[8,960,128]{2,1,0:T(8,128)S(1)} %get-tuple-element.8.new_in, bf16[8,8,48]{2,1,0:T(8,128)(2,1)S(1)} %get-tuple-element.9.out_in), custom_call_target="tpu_custom_call" | custom-call | tf_op jit(solution)/shard_map/pallas_call | solution.py:677

commit v3 on v2

--- a/solution.py
+++ b/solution.py
@@ -18,6 +18,7 @@
 LOCAL = 15
 BC_FIRST = 27
 BC_SLOTS = 5
+LATE = 4
 X_LOW, X_HIGH = -5, 2
 MESH = pl.DeviceIdType.MESH
 F32 = jnp.float32
@@ -97,6 +98,7 @@
     psend,
     pslots,
     counts,
+    shared,
     small_sem,
     in_sem,
     y_send,
@@ -109,6 +111,9 @@
     p_recv,
     n_send,
     n_recv,
+    late_send,
+    t_send,
+    t_recv,
 ):
     seqs = xbc_ref.shape[0]
     rows = seqs * K
@@ -119,6 +124,9 @@
     first_z = BC_FIRST - (columns - 1) * ROW
     has_slot = z >= first_z
     is_source = has_slot & (y == columns - 1)
+    is_late = (y == columns - 1) & (z == LATE)
+    feeds_late = (y == 0) & (z == LATE)
+    is_root = me == 0
     kind = lax.rem(me, 4)
     slot = jnp.maximum(z - first_z, 0)
 
@@ -150,9 +158,13 @@
 
     for other in range(first_z, ROW):
 
-        @pl.when(z != other)
+        @pl.when((z != other) & ((y != columns - 1) | (z != LATE) | (other == LATE)))
         def _():
             greet(sq, y * ROW + other)
+
+    @pl.when(is_late)
+    def _():
+        greet(sq, LATE)
 
     @pl.when(has_slot & (y != columns - 1))
     def _():
@@ -176,10 +188,18 @@
     def _():
         greet(sq, wrapped(me + 1, devices))
 
-    for step in range(1, groups):
-        greet(lax.rem(sq + step, groups), me)
-
-    expected = 7 * as_int(has_slot) + (columns - 1) * as_int(is_source) + groups
+    @pl.when(is_root)
+    def _():
+        for step in range(1, groups):
+            greet(lax.rem(sq + step, groups), me)
+
+    @pl.when(me != 0)
+    def _():
+        greet(sq, 0)
+
+    expected = (ROW - 1) * as_int(has_slot) + (columns - 1) * as_int(is_source) + 1
+    expected = expected - as_int(is_source & (z != LATE)) + as_int(feeds_late)
+    expected = expected + (devices + groups - 2) * as_int(is_root)
     for gap in range(X_LOW, X_HIGH + 1):
         if gap != 0:
             expected = expected + as_int(needs_values(wrapped(me - gap, devices), me))
@@ -220,78 +240,6 @@
     block = LOCAL // 3
     one_in_a, two_in_a = split > block, split > 2 * block
     has_zero_in_a = level_0 == 0
-
-    taken_here = jnp.int32(0)
-    for s in range(seqs):
-        taken_here = taken_here + acc_ref[s]
-    counts[sq] = jnp.full((8, 128), taken_here, jnp.int32).astype(F32)
-
-    pl.semaphore_wait(barrier, expected)
-
-    def remote(src, dst, send_sem, recv_sem, group, level):
-        return pltpu.make_async_remote_copy(
-            src_ref=src,
-            dst_ref=dst,
-            send_sem=send_sem,
-            recv_sem=recv_sem,
-            device_id=(group, level),
-            device_id_type=MESH,
-        )
-
-    def y_copy(row):
-        return remote(bc.at[slot], bc.at[slot], y_send.at[row], bc_recv.at[slot], sq, row * ROW + z)
-
-    def z_copy(step):
-        other = y * ROW + lax.rem(z + step, ROW)
-        return remote(bc.at[slot], bc.at[slot], z_send.at[step], bc_recv.at[slot], sq, other)
-
-    def x_copy(gap):
-        target = wrapped(me - gap, devices)
-        index = gap - X_LOW
-        return remote(piece, xs.at[index], x_send.at[index], x_recv.at[index], sq, target)
-
-    def low_copy():
-        target = wrapped(me + 1, devices)
-        return remote(low_send, low_recv, low_sems.at[0], low_sems.at[1], sq, target)
-
-    def count_copy(step):
-        return remote(
-            counts.at[sq], counts.at[sq], n_send.at[step], n_recv.at[sq], lax.rem(sq + step, groups), me
-        )
-
-    def partial_copy(index, gap):
-        target = wrapped(me + gap, devices)
-        return remote(psend.at[index], pslots.at[index], p_send.at[index], p_recv.at[index], sq, target)
-
-    sends_low = kind != 1
-    gets_low = kind != 2
-    gaps = [gap for gap in range(X_LOW, X_HIGH + 1) if gap != 0]
-    near = (
-        (0, 2, (kind == 0) | (kind == 3), (kind == 1) | (kind == 2)),
-        (1, 1, None, None),
-        (2, -1, kind == 3, kind == 2),
-    )
-
-    def when(cond, do):
-        if cond is None:
-            do()
-        else:
-            pl.when(cond)(do)
-
-    z_steps = (4, 3, 5, 2, 6, 1, 7)
-
-    @pl.when(is_source)
-    def _():
-        for r in range(columns - 1):
-            y_copy(r).start()
-        for step in z_steps:
-            z_copy(step).start()
-
-    for gap in gaps:
-        when(needs_values(wrapped(me - gap, devices), me), lambda: x_copy(gap).start())
-    for step in range(1, groups):
-        count_copy(step).start()
-
 
     for j in range(LOCAL):
         occupied = (pos_s >> levels[j]) & 1
@@ -319,7 +267,98 @@
         low_send[s] = jnp.where(has_zero_in_a, in_a, in_b).astype(BF16)
         return carry
 
-    lax.fori_loop(0, seqs, gather_low, 0)
+    @pl.when(z < first_z)
+    def _():
+        lax.fori_loop(0, seqs, gather_low, 0)
+
+    @pl.when(is_root)
+    def _():
+        taken_here = jnp.int32(0)
+        for s in range(seqs):
+            taken_here = taken_here + acc_ref[s]
+        counts[sq] = jnp.full((8, 128), taken_here, jnp.int32).astype(F32)
+
+    pl.semaphore_wait(barrier, expected)
+
+    def remote(src, dst, send_sem, recv_sem, group, level):
+        return pltpu.make_async_remote_copy(
+            src_ref=src,
+            dst_ref=dst,
+            send_sem=send_sem,
+            recv_sem=recv_sem,
+            device_id=(group, level),
+            device_id_type=MESH,
+        )
+
+    def y_copy(row):
+        return remote(bc.at[slot], bc.at[slot], y_send.at[row], bc_recv.at[slot], sq, row * ROW + z)
+
+    def z_copy(step):
+        other = y * ROW + lax.rem(z + step, ROW)
+        return remote(bc.at[slot], bc.at[slot], z_send.at[step], bc_recv.at[slot], sq, other)
+
+    def x_copy(gap):
+        target = wrapped(me - gap, devices)
+        index = gap - X_LOW
+        return remote(piece, xs.at[index], x_send.at[index], x_recv.at[index], sq, target)
+
+    def low_copy():
+        target = wrapped(me + 1, devices)
+        return remote(low_send, low_recv, low_sems.at[0], low_sems.at[1], sq, target)
+
+    def count_copy(step):
+        return remote(
+            counts.at[sq], counts.at[sq], n_send.at[step], n_recv.at[sq], lax.rem(sq + step, groups), me
+        )
+
+    others = [index for index in range(BC_SLOTS) if index != LATE - first_z]
+
+    def late_copy(index):
+        target = (columns - 1) * ROW + LATE
+        return remote(bc.at[index], bc.at[index], late_send.at[index], bc_recv.at[index], sq, target)
+
+    def total_copy(step):
+        return remote(shared, shared, t_send.at[step], t_recv.at[0], sq, step)
+
+    def partial_copy(index, gap):
+        target = wrapped(me + gap, devices)
+        return remote(psend.at[index], pslots.at[index], p_send.at[index], p_recv.at[index], sq, target)
+
+    sends_low = kind != 1
+    gets_low = kind != 2
+    gaps = [gap for gap in range(X_LOW, X_HIGH + 1) if gap != 0]
+    near = (
+        (0, 2, (kind == 0) | (kind == 3), (kind == 1) | (kind == 2)),
+        (1, 1, None, None),
+        (2, -1, kind == 3, kind == 2),
+    )
+
+    def when(cond, do):
+        if cond is None:
+            do()
+        else:
+            pl.when(cond)(do)
+
+    z_steps = (4, 3, 5, 2, 6, 1, 7)
+
+    @pl.when(is_source)
+    def _():
+        for r in range(columns - 1):
+            y_copy(r).start()
+        for step in z_steps:
+            when(lax.rem(z + step, ROW) != LATE, lambda: z_copy(step).start())
+
+    for gap in gaps:
+        when(needs_values(wrapped(me - gap, devices), me), lambda: x_copy(gap).start())
+    @pl.when(is_root)
+    def _():
+        for step in range(1, groups):
+            count_copy(step).start()
+
+
+    @pl.when(has_slot)
+    def _():
+        lax.fori_loop(0, seqs, gather_low, 0)
 
     when(sends_low, lambda: low_copy().start())
 
@@ -389,38 +428,75 @@
         wide_w[s] = jnp.where((lane[: LOCAL + 1] >> 3) == s, by_level, 0.0)
     parts[...] = jnp.zeros_like(parts)
 
-    for other in range(first_z, ROW):
-        index = other - first_z
-
-        @pl.when(z != other)
-        def _():
+    @pl.when(is_root)
+    def _():
+        for step in range(1, groups):
+            other = lax.rem(sq + step, groups)
             remote(
-                bc.at[index], bc.at[index], y_send.at[0], bc_recv.at[index], sq, me
+                counts.at[other], counts.at[other], n_send.at[step], n_recv.at[other], sq, me
             ).wait_recv()
-
-    got = [bc[i].astype(F32) for i in range(BC_SLOTS)]
-
-    def vectors(first_feature):
+        shared[...] = jnp.sum(counts[...], axis=0)
+        for step in range(1, devices):
+            total_copy(step).start()
+
+    def await_pieces(indices):
+        for index in indices:
+
+            @pl.when(z != first_z + index)
+            def _():
+                remote(
+                    bc.at[index], bc.at[index], y_send.at[0], bc_recv.at[index], sq, me
+                ).wait_recv()
+
+        for index in indices:
+            if index in others:
+
+                @pl.when(feeds_late)
+                def _():
+                    late_copy(index).start()
+
+    def vectors(first_feature, indices):
         pair = []
+        got = [bc[i].astype(F32) for i in indices]
         for r in range(2):
             part = jnp.zeros((half_rows, 128), F32)
-            for i in range(BC_SLOTS):
+            for i, moved in zip(indices, got):
                 start = OWN_IN * (BC_FIRST + i) - first_feature
-                if start > -OWN_IN and start < N:
-                    moved = got[i]
-                    by = (start - P_SIZE * r) % 128
-                    if by:
-                        moved = pltpu.roll(moved, by, 1)
-                    part = jnp.where((half_lane >= start) & (half_lane < start + OWN_IN), moved, part)
+                by = (start - P_SIZE * r) % 128
+                if by:
+                    moved = pltpu.roll(moved, by, 1)
+                part = jnp.where((half_lane >= start) & (half_lane < start + OWN_IN), moved, part)
             pair.append(part)
         return jnp.concatenate(pair, axis=0)
 
-    in_vecs = vectors(H * P_SIZE)
-    out_vecs = vectors(H * P_SIZE + N)
+    await_pieces((2, 3, 4))
+    out_vecs = vectors(H * P_SIZE + N, (2, 3, 4))
     across = jnp.transpose(jnp.concatenate([out_vecs, jnp.zeros_like(out_vecs)], axis=0))
     across = across.astype(BF16)
     cc[0:N, :] = across
     cc[N : 2 * N, :] = across
+
+    def read_out(s, carry):
+        size = block * P_SIZE
+        for part in range(3):
+            read = jnp.dot(
+                halves[s, part * size : (part + 1) * size, :], cc[...], preferred_element_type=F32
+            )
+            total = parts[part]
+            for i in range(block):
+                j = part * block + i
+                total = total + read[i * P_SIZE : (i + 1) * P_SIZE, :] * wide_w[s, j : j + 1, :]
+            parts[part] = total
+        return carry
+
+    lax.fori_loop(0, seqs, read_out, 0, unroll=2)
+
+    zero = jnp.zeros((P_SIZE, 128), F32)
+    in_a = parts[0] + jnp.where(one_in_a, parts[1], zero) + jnp.where(two_in_a, parts[2], zero)
+    in_b = jnp.where(one_in_a, zero, parts[1]) + jnp.where(two_in_a, zero, parts[2])
+    readout = jnp.transpose(jnp.concatenate([in_a, in_b], axis=0))[:rows]
+    await_pieces((0, 1))
+    in_vecs = vectors(H * P_SIZE, (0, 1, 2))
 
     for gap in gaps:
         index = gap - X_LOW
@@ -468,25 +544,6 @@
     zero_here = jnp.where(lower, 1, 0) == as_int(has_zero_in_a)
     drafts = jnp.where(zero_here, mixed * weight_zero, 0.0)
 
-    def read_out(s, carry):
-        size = block * P_SIZE
-        for part in range(3):
-            read = jnp.dot(
-                halves[s, part * size : (part + 1) * size, :], cc[...], preferred_element_type=F32
-            )
-            total = parts[part]
-            for i in range(block):
-                j = part * block + i
-                total = total + read[i * P_SIZE : (i + 1) * P_SIZE, :] * wide_w[s, j : j + 1, :]
-            parts[part] = total
-        return carry
-
-    lax.fori_loop(0, seqs, read_out, 0, unroll=2)
-
-    zero = jnp.zeros((P_SIZE, 128), F32)
-    in_a = parts[0] + jnp.where(one_in_a, parts[1], zero) + jnp.where(two_in_a, parts[2], zero)
-    in_b = jnp.where(one_in_a, zero, parts[1]) + jnp.where(two_in_a, zero, parts[2])
-    readout = jnp.transpose(jnp.concatenate([in_a, in_b], axis=0))[:rows]
     features = readout + drafts
     held_end = P_SIZE * heads_of(me)
 
@@ -560,13 +617,11 @@
     total = jnp.concatenate([total, pltpu.roll(total, P_SIZE, 1)], axis=0)
     out_ref[...] = total.reshape(seqs, K, 128)[:, :, 0:OWN_OUT].astype(BF16)
 
-    for step in range(1, groups):
-        other = lax.rem(sq + step, groups)
-        remote(
-            counts.at[other], counts.at[other], n_send.at[step], n_recv.at[other], sq, me
-        ).wait_recv()
-    taken = jnp.sum(counts[...], axis=0)
-    share_ref[...] = taken[0:1, 0:1] / (groups * seqs * K)
+    @pl.when(me != 0)
+    def _():
+        remote(shared, shared, t_send.at[0], t_recv.at[0], sq, me).wait_recv()
+
+    share_ref[...] = shared[0:1, 0:1] / (groups * seqs * K)
 
     @pl.when(is_source)
     def _():
@@ -576,13 +631,27 @@
     @pl.when(has_slot)
     def _():
         for step in range(1, ROW):
-            z_copy(step).wait_send()
+            when(
+                (y != columns - 1) | (lax.rem(z + step, ROW) != LATE),
+                lambda: z_copy(step).wait_send(),
+            )
+
+    @pl.when(feeds_late)
+    def _():
+        for index in others:
+            late_copy(index).wait_send()
 
     for gap in gaps:
         when(needs_values(wrapped(me - gap, devices), me), lambda: x_copy(gap).wait_send())
     when(sends_low, lambda: low_copy().wait_send())
-    for step in range(1, groups):
-        count_copy(step).wait_send()
+
+    @pl.when(is_root)
+    def _():
+        for step in range(1, groups):
+            count_copy(step).wait_send()
+        for step in range(1, devices):
+            total_copy(step).wait_send()
+
     for index, gap, sends, _ in near:
         when(sends, lambda: partial_copy(index, gap).wait_send())
 
@@ -644,6 +713,7 @@
             pltpu.VMEM((3, rows // 2, 128), F32),
             pltpu.VMEM((3, rows // 2, 128), F32),
             pltpu.VMEM((groups, 8, 128), F32),
+            pltpu.VMEM((8, 128), F32),
             dma((5,)),
             dma((seqs,)),
             dma((devices // ROW,)),
@@ -656,6 +726,9 @@
             dma((3,)),
             dma((groups,)),
             dma((groups,)),
+            dma((BC_SLOTS,)),
+            dma((devices,)),
+            dma((1,)),
         ],
         compiler_params=pltpu.CompilerParams(
             collective_id=0, has_side_effects=True, vmem_limit_bytes=40 << 20

time: 28.6 us -> 27.2 us (0.951)
  Pallas kernels: 25.8 us -> 24.5 us
    pallas_call x1, Pallas kernels: 23.8 us -> 22.5 us  [on_device(): pl.pallas_call(functools.partial(kernel, devices, groups), out_shape=(jax...]
where the time goes in v3:
time: 27.2 us; the launch traced here: 26.9 us
  Pallas kernels  24.5 us (90%)
  between operations  2.41 us (9%)
    pallas_call x1, Pallas kernels, on_device(): pl.pallas_call(functools.partial(kernel, devices, groups), out_shape=(jax...  22.5 us
    pallas_call x1, Pallas kernels, on_device(): pl.pallas_call(flush, out_shape=(jax.ShapeDtypeStruct(new_states.shape, F...  2 us

profile of v3, /device:TPU:10, one launch (start us, length us, event | category | flops | bytes accessed | tf_op | source)
XLA Modules:
  0.0 26.9 jit_solution(1563534148136502866)
XLA Ops:
  0.6 22.5 %shard_map.85 = (bf16[8,8,48]{2,1,0:T(8,128)(2,1)S(1)}, f32[8,960,128]{2,1,0:T(8,128)S(1)}, f32[1,1]{1,0:T(1,128)}) custom-call(f32[8,960,128]{2,1,0:T(8,128)} %bitcast.3, bf16[8,8,56]{2,1,0:T(8,128)(2,1)} %xbc_in.1, f32[8,8,24]{2,1,0:T(8,128)} %rates_in.1, f32[8,8,15]{2,1,0:T(8,128)} %weights_in.1, s32[8]{0:T(128)} %pos_in.1, s32[8]{0:T(128)} %acc_in.1), custom_call_target="tpu_custom_call" | custom-call | tf_op jit(solution)/shard_map/pallas_call | solution.py:680
  23.1 2.0 %shard_map.86 = (f32[8,960,128]{2,1,0:T(8,128)}, bf16[8,8,48]{2,1,0:T(8,128)(2,1)}) custom-call(f32[8,960,128]{2,1,0:T(8,128)S(1)} %get-tuple-element.8.new_in, bf16[8,8,48]{2,1,0:T(8,128)(2,1)S(1)} %get-tuple-element.9.out_in), custom_call_target="tpu_custom_call" | custom-call | tf_op jit(solution)/shard_map/pallas_call | solution.py:750

commit v4 on v3

--- a/solution.py
+++ b/solution.py
@@ -193,13 +193,18 @@
         for step in range(1, groups):
             greet(lax.rem(sq + step, groups), me)
 
-    @pl.when(me != 0)
+    @pl.when((z == 0) & (y != 0))
     def _():
         greet(sq, 0)
+
+    @pl.when(z != 0)
+    def _():
+        greet(sq, y * ROW)
 
     expected = (ROW - 1) * as_int(has_slot) + (columns - 1) * as_int(is_source) + 1
     expected = expected - as_int(is_source & (z != LATE)) + as_int(feeds_late)
-    expected = expected + (devices + groups - 2) * as_int(is_root)
+    expected = expected + (columns + groups - 2) * as_int(is_root)
+    expected = expected + (ROW - 1) * as_int(z == 0)
     for gap in range(X_LOW, X_HIGH + 1):
         if gap != 0:
             expected = expected + as_int(needs_values(wrapped(me - gap, devices), me))
@@ -317,8 +322,14 @@
         target = (columns - 1) * ROW + LATE
         return remote(bc.at[index], bc.at[index], late_send.at[index], bc_recv.at[index], sq, target)
 
-    def total_copy(step):
-        return remote(shared, shared, t_send.at[step], t_recv.at[0], sq, step)
+    def column_copy(r):
+        return remote(shared, shared, t_send.at[ROW + r], t_recv.at[0], sq, r * ROW)
+
+    def row_copy(step):
+        return remote(shared, shared, t_send.at[step], t_recv.at[0], sq, y * ROW + step)
+
+    def await_total():
+        remote(shared, shared, t_send.at[0], t_recv.at[0], sq, me).wait_recv()
 
     def partial_copy(index, gap):
         target = wrapped(me + gap, devices)
@@ -427,76 +438,6 @@
     for s in range(seqs):
         wide_w[s] = jnp.where((lane[: LOCAL + 1] >> 3) == s, by_level, 0.0)
     parts[...] = jnp.zeros_like(parts)
-
-    @pl.when(is_root)
-    def _():
-        for step in range(1, groups):
-            other = lax.rem(sq + step, groups)
-            remote(
-                counts.at[other], counts.at[other], n_send.at[step], n_recv.at[other], sq, me
-            ).wait_recv()
-        shared[...] = jnp.sum(counts[...], axis=0)
-        for step in range(1, devices):
-            total_copy(step).start()
-
-    def await_pieces(indices):
-        for index in indices:
-
-            @pl.when(z != first_z + index)
-            def _():
-                remote(
-                    bc.at[index], bc.at[index], y_send.at[0], bc_recv.at[index], sq, me
-                ).wait_recv()
-
-        for index in indices:
-            if index in others:
-
-                @pl.when(feeds_late)
-                def _():
-                    late_copy(index).start()
-
-    def vectors(first_feature, indices):
-        pair = []
-        got = [bc[i].astype(F32) for i in indices]
-        for r in range(2):
-            part = jnp.zeros((half_rows, 128), F32)
-            for i, moved in zip(indices, got):
-                start = OWN_IN * (BC_FIRST + i) - first_feature
-                by = (start - P_SIZE * r) % 128
-                if by:
-                    moved = pltpu.roll(moved, by, 1)
-                part = jnp.where((half_lane >= start) & (half_lane < start + OWN_IN), moved, part)
-            pair.append(part)
-        return jnp.concatenate(pair, axis=0)
-
-    await_pieces((2, 3, 4))
-    out_vecs = vectors(H * P_SIZE + N, (2, 3, 4))
-    across = jnp.transpose(jnp.concatenate([out_vecs, jnp.zeros_like(out_vecs)], axis=0))
-    across = across.astype(BF16)
-    cc[0:N, :] = across
-    cc[N : 2 * N, :] = across
-
-    def read_out(s, carry):
-        size = block * P_SIZE
-        for part in range(3):
-            read = jnp.dot(
-                halves[s, part * size : (part + 1) * size, :], cc[...], preferred_element_type=F32
-            )
-            total = parts[part]
-            for i in range(block):
-                j = part * block + i
-                total = total + read[i * P_SIZE : (i + 1) * P_SIZE, :] * wide_w[s, j : j + 1, :]
-            parts[part] = total
-        return carry
-
-    lax.fori_loop(0, seqs, read_out, 0, unroll=2)
-
-    zero = jnp.zeros((P_SIZE, 128), F32)
-    in_a = parts[0] + jnp.where(one_in_a, parts[1], zero) + jnp.where(two_in_a, parts[2], zero)
-    in_b = jnp.where(one_in_a, zero, parts[1]) + jnp.where(two_in_a, zero, parts[2])
-    readout = jnp.transpose(jnp.concatenate([in_a, in_b], axis=0))[:rows]
-    await_pieces((0, 1))
-    in_vecs = vectors(H * P_SIZE, (0, 1, 2))
 
     for gap in gaps:
         index = gap - X_LOW
@@ -522,6 +463,96 @@
         value_parts.append(part)
     values = jnp.concatenate(value_parts, axis=0)
 
+    turned = pltpu.roll(values, P_SIZE, 1)
+    values_a = jnp.where(lower, values, turned) * decay_a
+    values_b = jnp.where(lower, turned, values) * decay_b
+    for q in range(quads):
+        level, in_a, real = of_lane(q)
+        until = new_rows >> level
+        inside = ((until & 1) == 1) & ((token_rows >> level) + 1 == until) & live & real
+        term = jnp.where(inside, jnp.where(in_a, values_a, values_b), 0.0)
+        high, low = split_two(term)
+        both = jnp.concatenate(
+            [high.reshape(seqs, K, 128), low.reshape(seqs, K, 128)], axis=1
+        )
+        xg[:, :, q * 128 : (q + 1) * 128] = both.astype(BF16)
+
+    @pl.when(is_root)
+    def _():
+        for step in range(1, groups):
+            other = lax.rem(sq + step, groups)
+            remote(
+                counts.at[other], counts.at[other], n_send.at[step], n_recv.at[other], sq, me
+            ).wait_recv()
+        shared[...] = jnp.sum(counts[...], axis=0)
+        for r in range(1, columns):
+            column_copy(r).start()
+
+    @pl.when(z == 0)
+    def _():
+        pl.when(y != 0)(await_total)
+        for step in range(1, ROW):
+            row_copy(step).start()
+
+    def await_pieces(indices):
+        for index in indices:
+
+            @pl.when(z != first_z + index)
+            def _():
+                remote(
+                    bc.at[index], bc.at[index], y_send.at[0], bc_recv.at[index], sq, me
+                ).wait_recv()
+
+        for index in indices:
+            if index in others:
+
+                @pl.when(feeds_late)
+                def _():
+                    late_copy(index).start()
+
+    def vectors(first_feature, indices):
+        pair = []
+        got = [bc[i].astype(F32) for i in indices]
+        for r in range(2):
+            part = jnp.zeros((half_rows, 128), F32)
+            for i, moved in zip(indices, got):
+                start = OWN_IN * (BC_FIRST + i) - first_feature
+                by = (start - P_SIZE * r) % 128
+                if by:
+                    moved = pltpu.roll(moved, by, 1)
+                part = jnp.where((half_lane >= start) & (half_lane < start + OWN_IN), moved, part)
+            pair.append(part)
+        return jnp.concatenate(pair, axis=0)
+
+    await_pieces((2, 3, 4))
+    out_vecs = vectors(H * P_SIZE + N, (2, 3, 4))
+    across = jnp.transpose(jnp.concatenate([out_vecs, jnp.zeros_like(out_vecs)], axis=0))
+    across = across.astype(BF16)
+    cc[0:N, :] = across
+    cc[N : 2 * N, :] = across
+
+    def read_out(s, carry):
+        size = block * P_SIZE
+        for part in range(3):
+            read = jnp.dot(
+                halves[s, part * size : (part + 1) * size, :], cc[...], preferred_element_type=F32
+            )
+            total = parts[part]
+            for i in range(block):
+                j = part * block + i
+                total = total + read[i * P_SIZE : (i + 1) * P_SIZE, :] * wide_w[s, j : j + 1, :]
+            parts[part] = total
+        return carry
+
+    lax.fori_loop(0, seqs, read_out, 0, unroll=2)
+
+    zero = jnp.zeros((P_SIZE, 128), F32)
+    in_a = parts[0] + jnp.where(one_in_a, parts[1], zero) + jnp.where(two_in_a, parts[2], zero)
+    in_b = jnp.where(one_in_a, zero, parts[1]) + jnp.where(two_in_a, zero, parts[2])
+    readout = jnp.transpose(jnp.concatenate([in_a, in_b], axis=0))[:rows]
+    await_pieces((0, 1))
+    in_vecs = vectors(H * P_SIZE, (0, 1, 2))
+
     b16 = in_vecs.astype(BF16)
     scores = lax.dot_general(
         out_vecs.astype(BF16),
@@ -556,28 +587,13 @@
         moved = jnp.where(wanted, moved, 0.0)
         return moved[:half_rows] + pltpu.roll(moved[half_rows:], P_SIZE, 1)
 
-    for index, gap, _, _ in near:
+    for index, gap, sends, _ in near:
         psend[index] = packed_for(gap)
-    for index, gap, sends, _ in near:
         when(sends, lambda: partial_copy(index, gap).start())
     own = packed_for(0)
 
-    turned = pltpu.roll(values, P_SIZE, 1)
-    values_a = jnp.where(lower, values, turned) * decay_a
-    values_b = jnp.where(lower, turned, values) * decay_b
     b3 = in_vecs.reshape(seqs, K, N)
     bb[...] = jnp.concatenate([b3, b3], axis=1).astype(BF16)
-    for q in range(quads):
-        level, in_a, real = of_lane(q)
-        until = new_rows >> level
-        inside = ((until & 1) == 1) & ((token_rows >> level) + 1 == until) & live & real
-        term = jnp.where(inside, jnp.where(in_a, values_a, values_b), 0.0)
-        high, low = split_two(term)
-        both = jnp.concatenate(
-            [high.reshape(seqs, K, 128), low.reshape(seqs, K, 128)], axis=1
-        )
-        xg[:, :, q * 128 : (q + 1) * 128] = both.astype(BF16)
-
     when(gets_low, lambda: low_copy().wait_recv())
 
     def update(s, carry):
@@ -617,10 +633,7 @@
     total = jnp.concatenate([total, pltpu.roll(total, P_SIZE, 1)], axis=0)
     out_ref[...] = total.reshape(seqs, K, 128)[:, :, 0:OWN_OUT].astype(BF16)
 
-    @pl.when(me != 0)
-    def _():
-        remote(shared, shared, t_send.at[0], t_recv.at[0], sq, me).wait_recv()
-
+    pl.when(z != 0)(await_total)
     share_ref[...] = shared[0:1, 0:1] / (groups * seqs * K)
 
     @pl.when(is_source)
@@ -649,8 +662,13 @@
     def _():
         for step in range(1, groups):
             count_copy(step).wait_send()
-        for step in range(1, devices):
-            total_copy(step).wait_send()
+        for r in range(1, columns):
+            column_copy(r).wait_send()
+
+    @pl.when(z == 0)
+    def _():
+        for step in range(1, ROW):
+            row_copy(step).wait_send()
 
     for index, gap, sends, _ in near:
         when(sends, lambda: partial_copy(index, gap).wait_send())
@@ -727,7 +745,7 @@
             dma((groups,)),
             dma((groups,)),
             dma((BC_SLOTS,)),
-            dma((devices,)),
+            dma((ROW + devices // ROW,)),
             dma((1,)),
         ],
         compiler_params=pltpu.CompilerParams(

time: 27.2 us -> 27.4 us (level)
  the two profiles are of different devices: /device:TPU:10 before, /device:TPU:2 now
where the time goes in v4:
time: 27.4 us; the launch traced here: 27.3 us
  Pallas kernels  24.9 us (91%)
  between operations  2.41 us (9%)
    pallas_call x1, Pallas kernels, on_device(): pl.pallas_call(functools.partial(kernel, devices, groups), out_shape=(jax...  22.9 us
    pallas_call x1, Pallas kernels, on_device(): pl.pallas_call(flush, out_shape=(jax.ShapeDtypeStruct(new_states.shape, F...  2 us

profile of v4, /device:TPU:2, one launch (start us, length us, event | category | flops | bytes accessed | tf_op | source)
XLA Modules:
  0.0 27.3 jit_solution(4249532680251129977)
XLA Ops:
  0.6 22.9 %shard_map.85 = (bf16[8,8,48]{2,1,0:T(8,128)(2,1)S(1)}, f32[8,960,128]{2,1,0:T(8,128)S(1)}, f32[1,1]{1,0:T(1,128)}) custom-call(f32[8,960,128]{2,1,0:T(8,128)} %bitcast.3, bf16[8,8,56]{2,1,0:T(8,128)(2,1)} %xbc_in.1, f32[8,8,24]{2,1,0:T(8,128)} %rates_in.1, f32[8,8,15]{2,1,0:T(8,128)} %weights_in.1, s32[8]{0:T(128)} %pos_in.1, s32[8]{0:T(128)} %acc_in.1), custom_call_target="tpu_custom_call" | custom-call | tf_op jit(solution)/shard_map/pallas_call | solution.py:698
  23.6 2.0 %shard_map.86 = (f32[8,960,128]{2,1,0:T(8,128)}, bf16[8,8,48]{2,1,0:T(8,128)(2,1)}) custom-call(f32[8,960,128]{2,1,0:T(8,128)S(1)} %get-tuple-element.8.new_in, bf16[8,8,48]{2,1,0:T(8,128)(2,1)S(1)} %get-tuple-element.9.out_in), custom_call_target="tpu_custom_call" | custom-call | tf_op jit(solution)/shard_map/pallas_call | solution.py:768

commit v5 on v3

--- a/solution.py
+++ b/solution.py
@@ -267,7 +267,7 @@
         low_send[s] = jnp.where(has_zero_in_a, in_a, in_b).astype(BF16)
         return carry
 
-    @pl.when(z < first_z)
+    @pl.when(jnp.logical_not(is_source))
     def _():
         lax.fori_loop(0, seqs, gather_low, 0)
 
@@ -356,7 +356,7 @@
             count_copy(step).start()
 
 
-    @pl.when(has_slot)
+    @pl.when(is_source)
     def _():
         lax.fori_loop(0, seqs, gather_low, 0)
 
@@ -477,19 +477,16 @@
     cc[N : 2 * N, :] = across
 
     def read_out(s, carry):
-        size = block * P_SIZE
+        read = jnp.dot(halves[s], cc[...], preferred_element_type=F32)
         for part in range(3):
-            read = jnp.dot(
-                halves[s, part * size : (part + 1) * size, :], cc[...], preferred_element_type=F32
-            )
             total = parts[part]
-            for i in range(block):
-                j = part * block + i
-                total = total + read[i * P_SIZE : (i + 1) * P_SIZE, :] * wide_w[s, j : j + 1, :]
+            for k in range(block):
+                j = part * block + k
+                total = total + read[j * P_SIZE : (j + 1) * P_SIZE, :] * wide_w[s, j : j + 1, :]
             parts[part] = total
         return carry
 
-    lax.fori_loop(0, seqs, read_out, 0, unroll=2)
+    lax.fori_loop(0, seqs, read_out, 0, unroll=4)
 
     zero = jnp.zeros((P_SIZE, 128), F32)
     in_a = parts[0] + jnp.where(one_in_a, parts[1], zero) + jnp.where(two_in_a, parts[2], zero)
@@ -656,10 +653,16 @@
         when(sends, lambda: partial_copy(index, gap).wait_send())
 
 
-def flush(new_in, out_in, new_out, out_out, sems):
-    pieces = new_in.shape[0]
-    copies = [pltpu.make_async_copy(out_in, out_out, sems.at[pieces])]
-    copies += [pltpu.make_async_copy(new_in.at[s], new_out.at[s], sems.at[s]) for s in range(pieces)]
+def flush(new_in, out_in, share_in, new_out, out_out, share_out, sems):
+    pieces = sems.shape[0] - 2
+    size = new_in.shape[0] // pieces
+    copies = [
+        pltpu.make_async_copy(share_in, share_out, sems.at[pieces]),
+        pltpu.make_async_copy(out_in, out_out, sems.at[pieces + 1]),
+    ]
+    for i in range(pieces):
+        at = pl.ds(i * size, size)
+        copies.append(pltpu.make_async_copy(new_in.at[at], new_out.at[at], sems.at[i]))
     for copy in copies:
         copy.start()
     for copy in copies:
@@ -747,17 +750,18 @@
         ]
     )
     anywhere = pl.BlockSpec(memory_space=pl.ANY)
-    new_states, outputs = pl.pallas_call(
+    new_states, outputs, share = pl.pallas_call(
         flush,
         out_shape=(
             jax.ShapeDtypeStruct(new_states.shape, F32),
             jax.ShapeDtypeStruct(outputs.shape, BF16),
+            jax.ShapeDtypeStruct(share.shape, F32),
         ),
-        in_specs=[anywhere, anywhere],
-        out_specs=(in_hbm, in_hbm),
-        scratch_shapes=[dma((seqs + 1,))],
+        in_specs=[anywhere, anywhere, anywhere],
+        out_specs=(in_hbm, in_hbm, in_hbm),
+        scratch_shapes=[dma((seqs // 2 + 2,))],
         compiler_params=pltpu.CompilerParams(vmem_limit_bytes=4 << 20),
-    )(new_states, outputs)
+    )(new_states, outputs, share)
     return outputs, new_states.reshape(states.shape), share.reshape(())
 
 

time: 27.2 us -> 25.8 us (0.949)
  between operations: 2.41 us -> 0.64 us
  Pallas kernels: 24.5 us -> 25.1 us
    pallas_call x1, Pallas kernels: 2 us -> 2.61 us  [on_device(): pl.pallas_call(flush, out_shape=(jax.ShapeDtypeStruct(new_states.shape, F...]
where the time goes in v5:
time: 25.8 us; the launch traced here: 25.7 us
  Pallas kernels  25.1 us (97%)
  between operations  0.64 us (2%)
    pallas_call x1, Pallas kernels, on_device(): pl.pallas_call(functools.partial(kernel, devices, groups), out_shape=(jax...  22.5 us
    pallas_call x1, Pallas kernels, on_device(): pl.pallas_call(flush, out_shape=(jax.ShapeDtypeStruct(new_states.shape, F...  2.61 us

profile of v5, /device:TPU:10, one launch (start us, length us, event | category | flops | bytes accessed | tf_op | source)
XLA Modules:
  0.0 25.7 jit_solution(789432622961706494)
XLA Ops:
  0.6 22.5 %shard_map.85 = (bf16[8,8,48]{2,1,0:T(8,128)(2,1)S(1)}, f32[8,960,128]{2,1,0:T(8,128)S(1)}, f32[1,1]{1,0:T(1,128)}) custom-call(f32[8,960,128]{2,1,0:T(8,128)} %bitcast.3, bf16[8,8,56]{2,1,0:T(8,128)(2,1)} %xbc_in.1, f32[8,8,24]{2,1,0:T(8,128)} %rates_in.1, f32[8,8,15]{2,1,0:T(8,128)} %weights_in.1, s32[8]{0:T(128)} %pos_in.1, s32[8]{0:T(128)} %acc_in.1), custom_call_target="tpu_custom_call" | custom-call | tf_op jit(solution)/shard_map/pallas_call | solution.py:683
  23.1 2.6 %shard_map.86 = (f32[8,960,128]{2,1,0:T(8,128)}, bf16[8,8,48]{2,1,0:T(8,128)(2,1)}, f32[1,1]{1,0:T(1,128)}) custom-call(f32[8,960,128]{2,1,0:T(8,128)S(1)} %get-tuple-element.9.new_in, bf16[8,8,48]{2,1,0:T(8,128)(2,1)S(1)} %get-tuple-element.10.out_in, f32[1,1]{1,0:T(1,128)} %get-tuple-element.11.share_in), custom_call_target="tpu_custom_call" | custom-call | tf_op jit(solution)/shard_map/pallas_call | solution.py:753

commit v6 on v5

--- a/solution.py
+++ b/solution.py
@@ -759,7 +759,7 @@
         ),
         in_specs=[anywhere, anywhere, anywhere],
         out_specs=(in_hbm, in_hbm, in_hbm),
-        scratch_shapes=[dma((seqs // 2 + 2,))],
+        scratch_shapes=[dma((seqs + 2,))],
         compiler_params=pltpu.CompilerParams(vmem_limit_bytes=4 << 20),
     )(new_states, outputs, share)
     return outputs, new_states.reshape(states.shape), share.reshape(())

time: 25.8 us -> 25.9 us (level)
  no operation moved by 1% of the time
where the time goes in v6:
time: 25.9 us; the launch traced here: 25.8 us
  Pallas kernels  25.1 us (97%)
  between operations  0.64 us (2%)
    pallas_call x1, Pallas kernels, on_device(): pl.pallas_call(functools.partial(kernel, devices, groups), out_shape=(jax...  22.5 us
    pallas_call x1, Pallas kernels, on_device(): pl.pallas_call(flush, out_shape=(jax.ShapeDtypeStruct(new_states.shape, F...  2.64 us

profile of v6, /device:TPU:10, one launch (start us, length us, event | category | flops | bytes accessed | tf_op | source)
XLA Modules:
  0.0 25.8 jit_solution(6886322934375310558)
XLA Ops:
  0.6 22.5 %shard_map.85 = (bf16[8,8,48]{2,1,0:T(8,128)(2,1)S(1)}, f32[8,960,128]{2,1,0:T(8,128)S(1)}, f32[1,1]{1,0:T(1,128)}) custom-call(f32[8,960,128]{2,1,0:T(8,128)} %bitcast.3, bf16[8,8,56]{2,1,0:T(8,128)(2,1)} %xbc_in.1, f32[8,8,24]{2,1,0:T(8,128)} %rates_in.1, f32[8,8,15]{2,1,0:T(8,128)} %weights_in.1, s32[8]{0:T(128)} %pos_in.1, s32[8]{0:T(128)} %acc_in.1), custom_call_target="tpu_custom_call" | custom-call | tf_op jit(solution)/shard_map/pallas_call | solution.py:683
  23.1 2.6 %shard_map.86 = (f32[8,960,128]{2,1,0:T(8,128)}, bf16[8,8,48]{2,1,0:T(8,128)(2,1)}, f32[1,1]{1,0:T(1,128)}) custom-call(f32[8,960,128]{2,1,0:T(8,128)S(1)} %get-tuple-element.9.new_in, bf16[8,8,48]{2,1,0:T(8,128)(2,1)S(1)} %get-tuple-element.10.out_in, f32[1,1]{1,0:T(1,128)} %get-tuple-element.11.share_in), custom_call_target="tpu_custom_call" | custom-call | tf_op jit(solution)/shard_map/pallas_call | solution.py:753
